TPU v7x, 256 devices: a whole 4x4x8 slice. The times are simulated.
256 devices in a mesh: row: 32 (over z_lo, y, x), col: 8 (over z_hi, core).
Axes of the slice: x: 4, y: 4, z: 8 (z_hi: 4, z_lo: 2; z = z_hi * 2 + z_lo), core: 2. Of those that a mesh axis runs over, the one named last changes fastest.
Arguments:
- positions: float32 [3, 14336], P(None, ('row', 'col')), as said below
- polarizability: float32 [14336], P(('row', 'col')), may hold values from 0.04 to 0.16
- seeds: float32 [3, 16, 14336], P(None, None, ('row', 'col')), may hold values from -6 to 6
- dipoles: float32 [3, 16, 14336], P(None, None, ('row', 'col')), may hold values from -1.8 to 1.8
- tile_mask: int32 [256, 256], P('row', 'col'), may hold values from 0 to 1, as said below
Outputs:
- adjoint_field: float32 [3, 16, 14336], P(None, None, ('row', 'col'))
- gradient: float32 [3, 14336], P(None, ('row', 'col'))
Inputs may be any that keep to these rules, and one draw needn't show every extreme that they name: `positions`: beads lie near distinct points of a unit cubic lattice, each coordinate within 0.3 of its point; the points fill a roughly spherical droplet, and the beads of one block are spatially compact clusters of neighbouring points. Read as m_ab = tile_mask[a, (b % 8) * 32 + b // 8], m_ab is 1 exactly when the axis-aligned boxes spanned by the lattice points of blocks a and b lie within a distance of 6 of each other; so the table is symmetric with ones on the diagonal.
All inputs are finite; a program needn't handle non-finite values.
Results may differ from a plain program's by a relative error of at most 0.0003.
Values sent between devices are 32-bit elements; how exact they have to be, the bound alone decides.
No kernel may reach another device: no remote copies, remote signals or barrier semaphores. Data moves between devices by JAX's collectives and lax.ppermute only.
A program may use at most 64 MiB of HBM per device.

v0:
```python
import jax
import jax.numpy as jnp
from jax import lax
from jax.sharding import PartitionSpec as P

THOLE_DAMPING = 0.39
HIGHEST = lax.Precision.HIGHEST


def cut_along(x, dim, devices):
    before, after = (x.shape[:dim], x.shape[dim + 1 :])
    return jnp.moveaxis(x.reshape(*before, devices, -1, *after), dim, 0)


def sent_and_summed(x, axis, dim):
    pieces = cut_along(x, dim, lax.axis_size(axis))
    arrived = lax.all_to_all(pieces, axis, split_axis=0, concat_axis=0, tiled=True)
    return arrived.sum(axis=0)


def rows_first(arrays, axis, dims):
    turned = [jnp.moveaxis(a, dim, 0) for a, dim in zip(arrays, dims)]
    widths = [t[0].size for t in turned]
    both = jnp.concatenate([t.reshape(-1, w) for t, w in zip(turned, widths)], axis=1)
    out = lax.all_gather(both, axis, axis=0, tiled=True)
    pieces = jnp.split(out, [sum(widths[:k]) for k in range(1, len(widths))], axis=1)
    return tuple(
        (
            jnp.moveaxis(b.reshape(-1, *t.shape[1:]), 0, dim)
            for b, t, dim in zip(pieces, turned, dims)
        )
    )


def from_everyone(x, axis):
    devices = lax.axis_size(axis)
    return lax.all_to_all(jnp.broadcast_to(x[None], (devices, *x.shape)), axis, 0, 0, tiled=True)


def laid_out(pieces, dim):
    dims = list(pieces.shape[1:])
    dims[dim] *= pieces.shape[0]
    return jnp.moveaxis(pieces, 0, dim).reshape(dims)


def gathered_copies(x, axis, dim):
    pieces = from_everyone(x, axis)
    return laid_out(pieces, dim)


def pair_terms(row_geom, col_geom, keep_mask):
    offset = row_geom[:3, :, None] - col_geom[:3, None, :]
    dist_sq = jnp.sum(offset * offset, axis=0)
    dist_sq = jnp.where(keep_mask > 0.0, dist_sq, 1.0)
    inverse = lax.rsqrt(dist_sq)
    damping = (
        THOLE_DAMPING * dist_sq * (dist_sq * inverse) * row_geom[3][:, None] * col_geom[3][None, :]
    )
    damp_exp = jnp.exp(-damping)
    inv_cube = keep_mask * inverse * inverse * inverse
    isotropic = (1.0 - damp_exp) * inv_cube
    radial = 3.0 * (1.0 - (1.0 + damping) * damp_exp) * inv_cube * inverse * inverse
    tensor = radial[None, None] * offset[:, None] * offset[None, :]
    return (tensor, isotropic)


def apply_rows(tensor, isotropic, vector):
    result = jnp.einsum("abij,bpj->api", tensor, vector, precision=HIGHEST)
    return result - jnp.einsum("ij,apj->api", isotropic, vector, precision=HIGHEST)


def apply_cols(tensor, isotropic, vector):
    result = jnp.einsum("abij,bpi->apj", tensor, vector, precision=HIGHEST)
    return result - jnp.einsum("ij,api->apj", isotropic, vector, precision=HIGHEST)


def split_rows(values, groups):
    shaped = values.reshape(values.shape[:-1] + (groups, values.shape[-1] // groups))
    return jnp.moveaxis(shaped, -2, 0)


def join_rows(values):
    shifted = jnp.moveaxis(values, 0, -2)
    return shifted.reshape(shifted.shape[:-2] + (-1,))


def local(positions, polarizability, seeds, dipoles, tile_mask):
    bead_count = positions.shape[1]
    probes = seeds.shape[1]
    row_count = lax.axis_size("row")
    col_count = lax.axis_size("col")
    row_at = lax.axis_index("row")
    col_at = lax.axis_index("col")
    span_cols = bead_count * row_count
    geometry = jnp.concatenate([positions, lax.rsqrt(polarizability)[None, :]], axis=0)
    start_vector = polarizability[None, None, :] * seeds
    col_slot = jnp.arange(span_cols, dtype=jnp.int32)
    col_group = col_slot // bead_count
    col_global = (col_group * col_count + col_at) * bead_count + col_slot % bead_count
    row_global = (row_at * col_count + jnp.arange(col_count, dtype=jnp.int32))[:, None] * bead_count
    row_global = row_global + jnp.arange(bead_count, dtype=jnp.int32)[None, :]
    selector = (col_group[None, :] == jnp.arange(row_count, dtype=jnp.int32)[:, None]).astype(
        jnp.float32
    )
    col_mask = jnp.dot(tile_mask.astype(jnp.float32), selector, precision=HIGHEST)
    keep_mask = col_mask[:, None, :] * (row_global[:, :, None] != col_global[None, None, :]).astype(
        jnp.float32
    )

    def sweep_cols(vector_rows_split, rows_split, geom_cols):

        def one_shard(running, inputs):
            geom_rows, keep_rows, vector_rows = inputs
            tensor, isotropic = pair_terms(geom_rows, geom_cols, keep_rows)
            return (running + apply_cols(tensor, isotropic, vector_rows), None)

        empty_sum = jnp.zeros((3, probes, span_cols), jnp.float32)
        partial_cols, ignored = lax.scan(
            one_shard, empty_sum, (rows_split, keep_mask, vector_rows_split)
        )
        return sent_and_summed(partial_cols, "row", 2)

    geom_rows_all, start_rows = rows_first((geometry, start_vector), "col", (1, 2))
    geom_cols, dipole_cols = rows_first((geometry, dipoles), "row", (1, 2))
    rows_split = split_rows(geom_rows_all, col_count)
    field_one = seeds + sweep_cols(split_rows(start_rows, col_count), rows_split, geom_cols)
    next_vector = polarizability[None, None, :] * field_one
    next_rows = gathered_copies(next_vector, "col", 2)
    field_two = seeds + sweep_cols(split_rows(next_rows, col_count), rows_split, geom_cols)
    adjoint = polarizability[None, None, :] * field_two
    adjoint_rows = gathered_copies(adjoint, "col", 2)

    def pair_score(geom_rows, geom_all, keep_rows, adjoint_one):
        tensor, isotropic = pair_terms(geom_rows, geom_all, keep_rows)
        return jnp.sum(adjoint_one * apply_rows(tensor, isotropic, dipole_cols))

    slopes = jax.grad(pair_score, argnums=(0, 1))

    def force_shard(running, inputs):
        geom_rows, keep_rows, adjoint_one = inputs
        slope_rows, slope_cols = slopes(geom_rows, geom_cols, keep_rows, adjoint_one)
        return (running + slope_cols[:3], slope_rows[:3])

    empty_force = jnp.zeros((3, span_cols), jnp.float32)
    force_cols, force_split = lax.scan(
        force_shard, empty_force, (rows_split, keep_mask, split_rows(adjoint_rows, col_count))
    )
    force_rows = join_rows(force_split)
    gradient = sent_and_summed(force_rows, "col", 1) + sent_and_summed(force_cols, "row", 1)
    return (field_two, gradient)


def solution(mesh):
    in_specs = (
        P(None, ("row", "col")),
        P(("row", "col")),
        P(None, None, ("row", "col")),
        P(None, None, ("row", "col")),
        P("row", "col"),
    )
    out_specs = (P(None, None, ("row", "col")), P(None, ("row", "col")))
    return jax.shard_map(local, mesh=mesh, in_specs=in_specs, out_specs=out_specs, check_vma=False)
```

profile of v0, /device:TPU:1, one launch (start us, length us, event | category | flops | bytes accessed | tf_op | source)
XLA Modules:
  0.0 371.4 jit_solution(5194163001965535177)
XLA Ops:
  3.7 73.9 %all_gather.7 = f32[1792,52]{1,0:T(8,128)S(1)} all-gather(f32[56,52]{1,0:T(8,128)S(1)} %copy.28), channel_id=1, replica_groups=mesh['row'=32,'col'=8] {'row'}, dimensions={0}, use_global_device_ids=true | all-gather | bytes 384384 | tf_op jit(solution)/shard_map/all_gather | solution.py:25
  78.1 31.7 %all_gather.6 = f32[448,52]{1,0:T(8,128)S(1)} all-gather(f32[56,52]{1,0:T(8,128)S(1)} %copy.25), channel_id=1, replica_groups=mesh['row'=32,'col'=8] {'col'}, dimensions={0}, use_global_device_ids=true | all-gather | bytes 104832 | tf_op jit(solution)/shard_map/all_gather | solution.py:25
  110.4 2.0 compare_select_fusion
  112.4 44.9 %while.35 = (s32[]{:T(128)}, f32[3,16,1792]{2,1,0:T(8,128)S(1)}, f32[8,3,16,56]{3,0,2,1:T(8,128)S(1)}, f32[8,56,1792]{2,1,0:T(8,128)}, f32[8,4,56]{2,1,0:T(4,128...) while((s32[]{:T(128)}, f32[3,16,1792]{2,1,0:T(8,128)S(1)}, ...), condition=%wide.region_2.3_spmd.clone, body=%wide.region_0.2_spmd.clone.sunk | while | flops 236888064 | bytes 9123691 | solution.py:118
  114.2 2.1 fusion.132
  119.9 2.1 fusion.132
  125.5 2.1 fusion.132
  131.1 2.1 fusion.132
  136.7 2.1 fusion.132
  142.3 2.1 fusion.132
  147.9 2.1 fusion.132
  153.6 2.1 fusion.132
  159.5 12.1 %all_to_all.30 = f32[32,1,2688]{2,1,0:T(1,128)S(1)} all-to-all(f32[32,1,2688]{2,1,0:T(1,128)S(1)} %reshape.386), channel_id=1, replica_groups=mesh['row'=32,'col'=8] {'row'}, dimensions={0} | all-to-all | bytes 688128 | tf_op jit(solution)/shard_map/all_to_all | solution.py:17
  175.1 6.4 %all-to-all-start.1 = ((f32[8,1,2688]{2,1,0:T(1,128)}), f32[8,1,2688]{2,1,0:T(1,128)S(1)}, u32[]{:S(2)}, u32[]{:S(2)}) async-start(f32[8,1,2688]{2,1,0:T(1,128)} %reshape.388), calls=%async_computation.1 | async-start | bytes 172032 | tf_op jit(solution)/shard_map/all_to_all | solution.py:37
  181.6 7.6 %all-to-all-done.1 = f32[8,1,2688]{2,1,0:T(1,128)S(1)} async-done(((f32[8,1,2688]{2,1,0:T(1,128)}), f32[8,1,2688]{2,1,0:T(1,128)S(1)}, u32[]{:S(2)}, u32[]{:S(2)}) %all-to-all-start.1) | async-done | bytes 86048 | tf_op jit(solution)/shard_map/all_to_all | solution.py:37
  190.1 44.6 %while.36 = (s32[]{:T(128)}, f32[3,16,1792]{2,1,0:T(8,128)S(1)}, f32[8,3,16,56]{3,2,1,0:T(8,128)S(1)}, f32[8,56,1792]{2,1,0:T(8,128)}, f32[8,4,56]{2,1,0:T(4,128...) while((s32[]{:T(128)}, f32[3,16,1792]{2,1,0:T(8,128)S(1)}, ...), condition=%wide.region_6.7_spmd.clone, body=%wide.region_4.6_spmd.clone.sunk | while | flops 236888064 | bytes 9131659 | solution.py:118
  191.9 2.0 fusion.138
  197.5 2.0 fusion.138
  203.1 2.0 fusion.138
  208.7 2.0 fusion.138
  214.2 2.0 fusion.138
  219.8 2.0 fusion.138
  225.4 2.0 fusion.138
  230.9 2.0 fusion.138
  236.8 12.2 %all_to_all.31 = f32[32,1,2688]{2,1,0:T(1,128)S(1)} all-to-all(f32[32,1,2688]{2,1,0:T(1,128)S(1)} %reshape.390), channel_id=1, replica_groups=mesh['row'=32,'col'=8] {'row'}, dimensions={0} | all-to-all | bytes 688128 | tf_op jit(solution)/shard_map/all_to_all | solution.py:17
  252.6 5.5 %all-to-all-start.3 = ((f32[8,1,2688]{2,1,0:T(1,128)}), f32[8,1,2688]{2,1,0:T(1,128)S(1)}, u32[]{:S(2)}, u32[]{:S(2)}) async-start(f32[8,1,2688]{2,1,0:T(1,128)} %reshape.392), calls=%async_computation.3 | async-start | bytes 172032 | tf_op jit(solution)/shard_map/all_to_all | solution.py:37
  258.7 7.0 %all-to-all-done.3 = f32[8,1,2688]{2,1,0:T(1,128)S(1)} async-done(((f32[8,1,2688]{2,1,0:T(1,128)}), f32[8,1,2688]{2,1,0:T(1,128)S(1)}, u32[]{:S(2)}, u32[]{:S(2)}) %all-to-all-start.3) | async-done | bytes 86048 | tf_op jit(solution)/shard_map/all_to_all | solution.py:37
  266.8 80.1 %while.37 = (s32[]{:T(128)}, f32[3,1792]{1,0:T(4,128)S(1)}, f32[8,3,56]{2,1,0:T(4,128)S(1)}, f32[8,56,1792]{2,1,0:T(8,128)}, f32[8,4,56]{2,1,0:T(4,128)S(1)}, /*...) while((s32[]{:T(128)}, f32[3,1792]{1,0:T(4,128)S(1)}, ...), condition=%wide.region_17.18_spmd.clone, body=%wide.region_8.17_spmd.clone.sunk | while | flops 248187520 | bytes 19899200 | solution.py:145
  268.6 3.7 fusion.142
  272.4 2.0 multiply_reduce_fusion.9
  278.6 3.7 fusion.142
  282.4 2.0 multiply_reduce_fusion.9
  288.6 3.7 fusion.142
  292.4 2.0 multiply_reduce_fusion.9
  298.6 3.7 fusion.142
  302.5 2.0 multiply_reduce_fusion.9
  308.6 3.7 fusion.142
  312.5 2.0 multiply_reduce_fusion.9
  318.6 3.7 fusion.142
  322.5 2.0 multiply_reduce_fusion.9
  328.6 3.7 fusion.142
  332.5 2.0 multiply_reduce_fusion.9
  338.6 3.7 fusion.142
  342.5 2.0 multiply_reduce_fusion.9
  347.5 4.3 %all-to-all-start.4 = ((f32[8,1,168]{2,1,0:T(1,128)}), f32[8,1,168]{2,1,0:T(1,128)S(1)}, u32[]{:S(2)}, u32[]{:S(2)}) async-start(f32[8,1,168]{2,1,0:T(1,128)} %reshape.394), calls=%async_computation.4 | async-start | bytes 16384 | tf_op jit(solution)/shard_map/all_to_all | solution.py:17
  352.7 6.2 %all-to-all-done.4 = f32[8,1,168]{2,1,0:T(1,128)S(1)} async-done(((f32[8,1,168]{2,1,0:T(1,128)}), f32[8,1,168]{2,1,0:T(1,128)S(1)}, u32[]{:S(2)}, u32[]{:S(2)}) %all-to-all-start.4) | async-done | bytes 5408 | tf_op jit(solution)/shard_map/all_to_all | solution.py:17
  358.9 3.9 %all-to-all-start.5 = ((f32[32,1,168]{2,1,0:T(1,128)}), f32[32,1,168]{2,1,0:T(1,128)S(1)}, u32[]{:S(2)}, u32[]{:S(2)}) async-start(f32[32,1,168]{2,1,0:T(1,128)} %reshape.396), calls=%async_computation.5 | async-start | bytes 65536 | tf_op jit(solution)/shard_map/all_to_all | solution.py:17
  363.5 6.4 %all-to-all-done.5 = f32[32,1,168]{2,1,0:T(1,128)S(1)} async-done(((f32[32,1,168]{2,1,0:T(1,128)}), f32[32,1,168]{2,1,0:T(1,128)S(1)}, u32[]{:S(2)}, u32[]{:S(2)}) %all-to-all-start.5) | async-done | bytes 21536 | tf_op jit(solution)/shard_map/all_to_all | solution.py:17
  (319 shorter events, 111.5 us)
Async XLA Ops:
  77.7 32.6 %copy-start.2 = (s32[8,32]{1,0:T(8,128)S(1)}, s32[8,32]{1,0:T(8,128)}, u32[]{:S(2)}) copy-start(s32[8,32]{1,0:T(8,128)} %param.15) | copy-start | bytes 3076
  172.1 2.1 copy-start
  172.1 2.2 copy-start.1
  175.1 14.0 %all-to-all-start.1 = ((f32[8,1,2688]{2,1,0:T(1,128)}), f32[8,1,2688]{2,1,0:T(1,128)S(1)}, u32[]{:S(2)}, u32[]{:S(2)}) async-start(f32[8,1,2688]{2,1,0:T(1,128)} %reshape.388), calls=%async_computation.1 | async-start | bytes 172032 | tf_op jit(solution)/shard_map/all_to_all | solution.py:37
  252.6 13.1 %all-to-all-start.3 = ((f32[8,1,2688]{2,1,0:T(1,128)}), f32[8,1,2688]{2,1,0:T(1,128)S(1)}, u32[]{:S(2)}, u32[]{:S(2)}) async-start(f32[8,1,2688]{2,1,0:T(1,128)} %reshape.392), calls=%async_computation.3 | async-start | bytes 172032 | tf_op jit(solution)/shard_map/all_to_all | solution.py:37
  347.5 11.3 %all-to-all-start.4 = ((f32[8,1,168]{2,1,0:T(1,128)}), f32[8,1,168]{2,1,0:T(1,128)S(1)}, u32[]{:S(2)}, u32[]{:S(2)}) async-start(f32[8,1,168]{2,1,0:T(1,128)} %reshape.394), calls=%async_computation.4 | async-start | bytes 16384 | tf_op jit(solution)/shard_map/all_to_all | solution.py:17
  358.9 11.1 %all-to-all-start.5 = ((f32[32,1,168]{2,1,0:T(1,128)}), f32[32,1,168]{2,1,0:T(1,128)S(1)}, u32[]{:S(2)}, u32[]{:S(2)}) async-start(f32[32,1,168]{2,1,0:T(1,128)} %reshape.396), calls=%async_computation.5 | async-start | bytes 65536 | tf_op jit(solution)/shard_map/all_to_all | solution.py:17
where the time goes:
time: 374 us; the launch traced here: 371 us
  blocking collectives  130 us (35%)
  matrix products  105 us (28%)
  other arithmetic  72.7 us (19%)
  waiting for transfers between devices  27.2 us (7%)
  starting transfers between devices  20.1 us (5%)
  local copies, waits for them, and re-layouts  13.2 us (4%)
    all_gather x2, blocking collectives, rows_first(): out = lax.all_gather(both, axis, axis=0, tiled=True)  106 us
    dot_general x16, matrix products, apply_cols(): result = jnp.einsum('abij,bpi->apj', tensor, vector, precision=HIGHEST)  32.8 us
    mul x24, other arithmetic, pair_terms(): 3.0 * (1.0 - (1.0 + damping) * damp_exp) * inv_cube * inverse * inverse  31 us
    dot_general x8, matrix products, apply_rows(): result = jnp.einsum('abij,bpj->api', tensor, vector, precision=HIGHEST)  29.3 us
    dot_general x16, matrix products, apply_cols(): jnp.einsum('ij,api->apj', isotropic, vector, precision=HIGHEST)  27.4 us
    all_to_all x2, blocking collectives, sent_and_summed(): lax.all_to_all(pieces, axis, split_axis=0, concat_axis=0, tiled=True)  24.3 us
    dot_general x8, matrix products, apply_rows(): jnp.einsum('ij,apj->api', isotropic, vector, precision=HIGHEST)  15.7 us
    all_to_all x2, waiting for transfers between devices, from_everyone(): lax.all_to_all(jnp.broadcast_to(x[None], (devices, *x.shape)), axis, 0, 0...  14.6 us
  transfers between devices with their start and end apart: 4, of which 4 were waited for; matrix products, arithmetic and copies ran while one was open for 1% of the time, Pallas kernels for 0%

commit v1 on v0

v1 whole, which is shorter than its diff:
```python
import jax
import jax.numpy as jnp
from jax import lax
from jax.experimental import pallas as pl
from jax.experimental.pallas import tpu as pltpu
from jax.sharding import PartitionSpec as P

THOLE_DAMPING = 0.39
HIGHEST = lax.Precision.HIGHEST
F32 = jnp.float32
BF16 = jnp.bfloat16

BEAD = 56
NROW = 32
NCOL = 8
RB = NCOL * BEAD
CB = NROW * BEAD
LANE = 128
PAIRS = ((0, 0), (1, 1), (2, 2), (0, 1), (0, 2), (1, 2))
VMEM_SPEC = pl.BlockSpec(memory_space=pltpu.VMEM)


def dot_f32(a, b, dims, precision=None):
    return lax.dot_general(a, b, (dims, ((), ())), precision=precision, preferred_element_type=F32)


def hi_lo(x):
    hi = x.astype(BF16).astype(F32)
    return hi, x - hi


def lane_ids(shape):
    return lax.broadcasted_iota(jnp.int32, shape, 1)


def arranged(u, a, b):
    group = (lane_ids(u.shape) % 64) // 16
    if a == b:
        return jnp.where(group == a, u, 0.0)
    step = 16 * (b - a)
    down = pltpu.roll(u, LANE - step, 1)
    up = pltpu.roll(u, step, 1)
    return jnp.where(group == a, down, jnp.where(group == b, up, 0.0))


def build_kernel(gc_ref, gr_ref, mask_ref, t_ref, f5_ref, g7_ref, xc_ref, y_ref, w_ref, m_ref):
    for k in range(CB // 256):
        rows = pl.ds(k * 256, 256)
        g = gc_ref[rows, :]
        pick = (lane_ids((8, LANE)) == 96 + lax.broadcasted_iota(jnp.int32, (8, LANE), 0)).astype(F32)
        xc_ref[:, rows] = dot_f32(pick, g, ((1,), (1,)), HIGHEST)
        v = jnp.where(lane_ids(g.shape) < 48, g, 0.0)
        hi, lo = hi_lo(v)
        u = hi + pltpu.roll(lo, 64, 1)
        for n, (a, b) in enumerate(PAIRS):
            w_ref[n, rows, :] = arranged(u, a, b).astype(BF16)
    block = lax.broadcasted_iota(jnp.int32, (NROW, CB), 1) // BEAD
    owner = lax.broadcasted_iota(jnp.int32, (NROW, CB), 0)
    chosen = (block == owner).astype(BF16)
    keep_all = dot_f32(mask_ref[...].astype(F32).astype(BF16), chosen, ((1,), (0,)))
    for k in range(NCOL):
        m_ref[k] = jnp.broadcast_to(keep_all[k : k + 1], (8, CB))

    def row_chunk(q, carry):
        r0 = pl.multiple_of(q * 16, 16)
        rows = pl.ds(r0, 16)
        g = gr_ref[rows, :]
        xr, yr, zr, sr = (jnp.broadcast_to(g[:, 96 + k : 97 + k], (16, LANE)) for k in range(4))
        sr = sr * THOLE_DAMPING
        first = (2 * q) // 7
        second = (2 * q + 1) // 7
        for k in range(CB // LANE):
            cols = pl.ds(k * LANE, LANE)
            row_of = lambda i: jnp.broadcast_to(xc_ref[i : i + 1, cols], (16, LANE))
            keep = jnp.concatenate(
                [
                    m_ref[first, :, cols],
                    m_ref[second, :, cols],
                ],
                axis=0,
            )
            dx, dy, dz = xr - row_of(0), yr - row_of(1), zr - row_of(2)
            r2 = dx * dx + dy * dy + dz * dz
            inv = lax.rsqrt(jnp.maximum(r2, 1e-12)) * keep
            v = (r2 * (r2 * inv)) * (sr * row_of(3))
            e = jnp.exp(-v)
            ve = v * e
            one = 1.0 - e
            inv2 = inv * inv
            inv3 = inv2 * inv
            f3 = one * inv3
            inv5 = inv3 * inv2
            f5 = ((one - ve) * 3.0) * inv5
            g7 = inv2 * ((v * ve) * inv5 * 9.0 - 5.0 * f5)
            f5_ref[rows, cols] = f5
            g7_ref[rows, cols] = g7
            fx, fy, fz = f5 * dx, f5 * dy, f5 * dz
            parts = (fx * dx - f3, fy * dy - f3, fz * dz - f3, fx * dy, fx * dz, fy * dz)
            for n, t in enumerate(parts):
                hi = t.astype(BF16)
                t_ref[n, rows, cols] = hi
                t_ref[6 + n, rows, cols] = (t - hi.astype(F32)).astype(BF16)
        return carry

    lax.fori_loop(0, RB // 16, row_chunk, 0)
    for q in range(4):
        rows = pl.ds(q * 112, 112)
        total = jnp.zeros((112, LANE), F32)
        for n in range(12):
            total += dot_f32(t_ref[n, rows, :], w_ref[n % 6], ((1,), (0,)))
        y = total + pltpu.roll(total, 64, 1)
        y_ref[rows, :] = y


def second_kernel(got_ref, gr_ref, t_ref, out_ref, w_ref, y_ref):
    y = got_ref[0]
    for k in range(1, NCOL):
        y = y + got_ref[k]
    y = jnp.concatenate([y, pltpu.roll(y, 64, 1)], axis=0)
    g = gr_ref[...]
    lanes = lane_ids((RB, LANE))
    pol = jnp.broadcast_to(g[:, 100:101], (RB, LANE))
    vec = jnp.where(lanes < 48, g + pol * y, 0.0)
    hi, lo = hi_lo(vec)
    u = hi + pltpu.roll(lo, 64, 1)
    ut = u.T
    group = (lax.broadcasted_iota(jnp.int32, (LANE, RB), 0) % 64) // 16
    for n, (a, b) in enumerate(PAIRS):
        if a == b:
            w = jnp.where(group == a, ut, 0.0)
        else:
            step = 16 * (b - a)
            down = jnp.concatenate([ut[step:], ut[:step]], axis=0)
            up = jnp.concatenate([ut[LANE - step :], ut[: LANE - step]], axis=0)
            w = jnp.where(group == a, down, jnp.where(group == b, up, 0.0))
        w_ref[n] = w.astype(BF16)
    for k in range(7):
        cols = pl.ds(k * 256, 256)
        total = jnp.zeros((LANE, 256), F32)
        for n in range(12):
            total += dot_f32(w_ref[n % 6], t_ref[n, :, cols], ((1,), (0,)))
        y_ref[:, cols] = total[0:48] + total[64:112]
    for j in range(NROW):
        out_ref[j, :, 0:BEAD] = y_ref[0:24, j * BEAD : (j + 1) * BEAD]
        out_ref[j, :, 64 : 64 + BEAD] = y_ref[24:48, j * BEAD : (j + 1) * BEAD]


def own_kernel(got_ref, seeds_ref, pol_ref, field_ref, next_ref):
    y = got_ref[0]
    for k in range(1, NROW):
        y = y + got_ref[k]
    y = jnp.concatenate([y, pltpu.roll(y, 64, 1)], axis=0)
    field = seeds_ref[...] + y[:, 0:BEAD]
    field_ref[...] = field
    vec = pol_ref[...] * field
    pad = jnp.concatenate([vec, jnp.zeros((48, LANE - BEAD), F32)], axis=1)
    pad = jnp.concatenate([pad, jnp.zeros((LANE - 48, LANE), F32)], axis=0)
    turned = pad.T
    next_ref[...] = turned[0:BEAD]


def gradient_kernel(
    a_ref, gc_ref, gr_ref, f5_ref, g7_ref, xc_ref, or_ref, oc_ref, l_ref, m_ref, h_ref, racc_ref, cacc_ref
):
    a = a_ref[...]
    ahi, alo = hi_lo(a)
    ahi = ahi + pltpu.roll(ahi, 64, 1)
    alo = alo + pltpu.roll(alo, 64, 1)
    for n, (p, q) in enumerate(PAIRS):
        scale = 2.0 if p == q else 1.0
        l_ref[n, :, 0:LANE] = (arranged(ahi, p, q) * scale).astype(BF16)
        l_ref[n, :, LANE:] = (arranged(alo, p, q) * scale).astype(BF16)
    for k in range(CB // 256):
        rows = pl.ds(k * 256, 256)
        g = gc_ref[rows, :]
        mu = jnp.where(lane_ids(g.shape) < 48, pltpu.roll(g, 80, 1), 0.0)
        hi, lo = hi_lo(mu)
        u = (hi + pltpu.roll(lo, 64, 1)).astype(BF16)
        m_ref[rows, 0:LANE] = u
        m_ref[rows, LANE:] = u
    racc_ref[...] = jnp.zeros_like(racc_ref)

    def col_chunk(k, carry):
        c0 = pl.multiple_of(k * 256, 256)
        cols = pl.ds(c0, 256)
        for n in range(6):
            h_ref[n] = dot_f32(l_ref[n], m_ref[cols, :], ((1,), (1,)))
        xc, yc, zc = (jnp.broadcast_to(xc_ref[i : i + 1, cols], (8, 256)) for i in range(3))

        def rows_step(t, acc):
            r0 = pl.multiple_of(t * 8, 8)
            rows = pl.ds(r0, 8)
            g = gr_ref[rows, :]
            xr, yr, zr = (jnp.broadcast_to(g[:, 96 + i : 97 + i], (8, 256)) for i in range(3))
            dx, dy, dz = xr - xc, yr - yc, zr - zc
            hxx, hyy, hzz, hxy, hxz, hyz = (h_ref[n, rows, :] for n in range(6))
            wx = hxx * dx + hxy * dy + hxz * dz
            wy = hxy * dx + hyy * dy + hyz * dz
            wz = hxz * dx + hyz * dy + hzz * dz
            f5 = f5_ref[rows, cols]
            e = g7_ref[rows, cols] * (wx * dx + wy * dy + wz * dz) + f5 * (hxx + hyy + hzz)
            f52 = f5 + f5
            out = []
            for i, (d, w) in enumerate(((dx, wx), (dy, wy), (dz, wz))):
                s = e * d + f52 * w
                racc_ref[i, rows, :] += s[:, 0:LANE] + s[:, LANE:]
                out.append(acc[i] + s)
            return tuple(out)

        zero = jnp.zeros((8, 256), F32)
        acc = lax.fori_loop(0, RB // 8, rows_step, (zero, zero, zero), unroll=2)
        for i in range(3):
            cacc_ref[i : i + 1, cols] = -0.5 * jnp.sum(acc[i], axis=0, keepdims=True)
        return carry

    lax.fori_loop(0, CB // 256, col_chunk, 0)
    ones = jnp.full((8, LANE), 0.5, F32)
    row = lax.broadcasted_iota(jnp.int32, (8, RB), 0)
    total = jnp.zeros((8, RB), F32)
    for i in range(3):
        part = dot_f32(ones, racc_ref[i], ((1,), (1,)), HIGHEST)
        total = jnp.where(row == i, part, total)
    racc_ref[0, 0:8, :] = total[:, 0:LANE]
    racc_ref[0, 8:16, :] = total[:, LANE : 2 * LANE]
    for j in range(NCOL):
        or_ref[j, :, 0:BEAD] = total[:, j * BEAD : (j + 1) * BEAD]
    for j in range(NROW):
        oc_ref[j, :, 0:BEAD] = cacc_ref[:, j * BEAD : (j + 1) * BEAD]


def final_kernel(rgot_ref, cgot_ref, out_ref):
    total = rgot_ref[0]
    for k in range(1, NCOL):
        total = total + rgot_ref[k]
    for k in range(NROW):
        total = total + cgot_ref[k]
    out_ref[...] = total[0:3, 0:BEAD]


def call(kernel, outs, scratch, flops, limit_mib):
    return pl.pallas_call(
        kernel,
        out_shape=[jax.ShapeDtypeStruct(s, t) for s, t in outs],
        out_specs=[VMEM_SPEC] * len(outs),
        scratch_shapes=[pltpu.VMEM(s, t) for s, t in scratch],
        compiler_params=pltpu.CompilerParams(vmem_limit_bytes=limit_mib << 20),
        cost_estimate=pl.CostEstimate(flops=flops, bytes_accessed=4_000_000, transcendentals=0),
    )


def run_build(gc, gr, mask):
    return call(
        build_kernel,
        [((12, RB, CB), BF16), ((RB, CB), F32), ((RB, CB), F32), ((8, CB), F32), ((RB, LANE), F32)],
        [((6, CB, LANE), BF16), ((NCOL, 8, CB), F32)],
        400_000_000,
        12,
    )(gc, gr, mask)


def run_second(got, gr, t):
    return call(
        second_kernel,
        [((NROW, 24, LANE), F32)],
        [((6, LANE, RB), BF16), ((48, CB), F32)],
        200_000_000,
        12,
    )(got, gr, t)[0]


def run_own(got, seeds, pol):
    return call(own_kernel, [((48, BEAD), F32), ((BEAD, LANE), F32)], [], 100_000, 4)(got, seeds, pol)


def run_gradient(a, gc, gr, f5, g7, xc):
    return call(
        gradient_kernel,
        [((NCOL, 8, LANE), F32), ((NROW, 8, LANE), F32)],
        [
            ((6, RB, 2 * LANE), BF16),
            ((CB, 2 * LANE), BF16),
            ((6, RB, 256), F32),
            ((3, RB, LANE), F32),
            ((8, CB), F32),
        ],
        300_000_000,
        12,
    )(a, gc, gr, f5, g7, xc)


def broadcast_all(x, axis):
    n = lax.axis_size(axis)
    return lax.all_to_all(jnp.broadcast_to(x[None], (n, *x.shape)), axis, 0, 0, tiled=True)


def exchange(x, axis):
    return lax.all_to_all(x, axis, 0, 0, tiled=True)


def local(positions, polarizability, seeds, dipoles, tile_mask):
    seeds = seeds.reshape(48, BEAD)
    dipoles = dipoles.reshape(48, BEAD)
    pol = polarizability[None, :]
    own = jnp.concatenate(
        [pol * seeds, dipoles, positions, lax.rsqrt(pol), pol, jnp.zeros((27, BEAD), F32)], axis=0
    ).T
    gc = broadcast_all(own, "row").reshape(CB, LANE)
    gr = broadcast_all(own, "col").reshape(RB, LANE)
    t, f5, g7, xc, y1 = run_build(gc, gr, tile_mask)
    half = jnp.concatenate([y1[: RB // 2, 0:64], y1[RB // 2 :, 0:64]], axis=1)
    got = broadcast_all(half, "col")
    got2 = exchange(run_second(got, gr, t), "row")
    field, nxt = run_own(got2, seeds, pol)
    a = broadcast_all(nxt, "col").reshape(RB, LANE)
    out_r, out_c = run_gradient(a, gc, gr, f5, g7, xc)
    rgot = exchange(out_r, "col")
    cgot = exchange(out_c, "row")
    (gradient,) = call(final_kernel, [((3, BEAD), F32)], [], 100_000, 4)(rgot, cgot)
    return (field.reshape(3, 16, BEAD), gradient)


def solution(mesh):
    in_specs = (
        P(None, ("row", "col")),
        P(("row", "col")),
        P(None, None, ("row", "col")),
        P(None, None, ("row", "col")),
        P("row", "col"),
    )
    out_specs = (P(None, None, ("row", "col")), P(None, ("row", "col")))
    return jax.shard_map(local, mesh=mesh, in_specs=in_specs, out_specs=out_specs, check_vma=False)
```

time: 374 us -> 173 us (0.46)
  matrix products: 105 us -> 0 us
  other arithmetic: 72.7 us -> 0.86 us
  Pallas kernels: 0 us -> 46.2 us
  waiting for transfers between devices: 27.2 us -> 0 us
  starting transfers between devices: 20.1 us -> 0 us
  local copies, waits for them, and re-layouts: 13.2 us -> 3.46 us
  blocking collectives: 130 us -> 121 us
    all_gather x2 -> x0, blocking collectives: 106 us -> none  [rows_first(): out = lax.all_gather(both, axis, axis=0, tiled=True)]
    dot_general x49 -> x0, matrix products: 105 us -> none  [the longest x16 32.8 us: apply_cols(): result = jnp.einsum('abij,bpi->apj', tensor, vector, precision=HIGHEST)]
    all_to_all x2 -> x7, blocking collectives: 24.3 us -> 121 us  [the longest x4 82.9 us: broadcast_all(): lax.all_to_all(jnp.broadcast_to(x[None], (n, *x.shape)), axis, 0, 0, tile...]
    pallas_call x0 -> x5, Pallas kernels: none -> 46.2 us  [the longest x1 24.5 us: run_gradient(): call(gradient_kernel, [((NCOL, 8, LANE), F32), ((NROW, 8, LANE), F32)], [...]
    mul x45 -> x1, other arithmetic: 38.1 us -> 0.76 us  [local(): pol * seeds]
    all_to_all x4 -> x0, waiting for transfers between devices: 27.2 us -> none  [the longest x2 14.6 us: from_everyone(): lax.all_to_all(jnp.broadcast_to(x[None], (devices, *x.shape)), axis, 0, 0...]
    all_to_all x4 -> x0, starting transfers between devices: 20.1 us -> none  [the longest x2 11.9 us: from_everyone(): lax.all_to_all(jnp.broadcast_to(x[None], (devices, *x.shape)), axis, 0, 0...]
    select_n x9 -> x0, other arithmetic: 13.8 us -> none  [the longest x8 13.8 us: pair_terms(): dist_sq = jnp.where(keep_mask > 0.0, dist_sq, 1.0)]
  transfers between devices with their start and end apart: 4 -> 0, of which waited for: 4 -> 0; matrix products, arithmetic and copies ran while one was open for 1% -> 0% of each run, Pallas kernels for 0% -> 0%
where the time goes in v1:
time: 173 us; the launch traced here: 172 us
  blocking collectives  121 us (70%)
  Pallas kernels  46.2 us (27%)
  local copies, waits for them, and re-layouts  3.46 us (2%)
    all_to_all x4, blocking collectives, broadcast_all(): lax.all_to_all(jnp.broadcast_to(x[None], (n, *x.shape)), axis, 0, 0, tile...  82.9 us
    all_to_all x3, blocking collectives, exchange(): return lax.all_to_all(x, axis, 0, 0, tiled=True)  38.2 us
    pallas_call x1, Pallas kernels, run_gradient(): call(gradient_kernel, [((NCOL, 8, LANE), F32), ((NROW, 8, LANE), F32)], [...  24.5 us
    pallas_call x1, Pallas kernels, run_build(): call(build_kernel, [((12, RB, CB), BF16), ((RB, CB), F32), ((RB, CB), F32...  16.9 us

profile of v1, /device:TPU:1, one launch (start us, length us, event | category | flops | bytes accessed | tf_op | source)
XLA Modules:
  0.0 172.3 jit_solution(14648337800282461596)
XLA Ops:
  0.6 0.0 copy-start.2
  0.6 0.7 rsqrt_bitcast_fusion
  1.3 0.8 broadcast_multiply_fusion
  2.1 0.1 copy.14
  2.1 0.1 copy.17
  2.2 0.8 copy.16
  3.0 0.8 copy.15
  3.8 0.7 copy.18
  4.6 0.1 concatenate.6
  4.7 18.7 %all_to_all.35 = f32[8,56,128]{2,1,0:T(8,128)S(1)} all-to-all(f32[8,56,128]{2,1,0:T(8,128)S(1)} %broadcast_in_dim.15), channel_id=1, replica_groups=mesh['row'=32,'col'=8] {'col'}, dimensions={0} | all-to-all | bytes 458752 | tf_op jit(solution)/shard_map/all_to_all | solution.py:293
  23.4 0.1 broadcast_in_dim.14
  23.5 20.2 %all_to_all.36 = f32[32,56,128]{2,1,0:T(8,128)S(1)} all-to-all(f32[32,56,128]{2,1,0:T(8,128)S(1)} %broadcast_in_dim.14), channel_id=1, replica_groups=mesh['row'=32,'col'=8] {'row'}, dimensions={0} | all-to-all | bytes 1835008 | tf_op jit(solution)/shard_map/all_to_all | solution.py:293
  43.7 0.0 copy-done.2
  43.7 16.9 %shard_map.68 = (bf16[12,448,1792]{2,1,0:T(8,128)(2,1)S(1)}, f32[448,1792]{1,0:T(8,128)S(1)}, f32[448,1792]{1,0:T(8,128)S(1)}, f32[8,1792]{1,0:T(8,128)S(1)}, f32[448,128]{1,0:T(8,128)S(1)}) custom-call(f32[1792,128]{1,0:T(8,128)S(1)} %bitcast.11, f32[448,128]{1,0:T(8,128)S(1)} %bitcast.13, s32[8,32]{1,0:T(8,128)S(1)} %copy-done.2), custom_call_target="tpu_custom_call" | custom-call | flops 400000000 | bytes 4000000 | tf_op jit(solution)/shard_map/pallas_call | solution.py:252
  60.7 0.1 pad_maximum_fusion
  60.8 0.1 broadcast_in_dim.16
  60.9 29.8 %all_to_all.37.got_ref = f32[8,224,128]{2,1,0:T(8,128)S(1)} all-to-all(f32[8,224,128]{2,1,0:T(8,128)S(1)} %broadcast_in_dim.16), channel_id=1, replica_groups=mesh['row'=32,'col'=8] {'col'}, dimensions={0} | all-to-all | bytes 1835008 | tf_op jit(solution)/shard_map/all_to_all | solution.py:293
  90.6 0.0 copy-start
  90.6 0.0 copy-start.1
  90.6 3.4 %shard_map.69 = f32[32,24,128]{2,1,0:T(8,128)S(1)} custom-call(f32[8,224,128]{2,1,0:T(8,128)S(1)} %all_to_all.37.got_ref, f32[448,128]{1,0:T(8,128)S(1)} %bitcast.14, bf16[12,448,1792]{2,1,0:T(8,128)(2,1)S(1)} %get-tuple-element.12.t_ref), custom_call_target="tpu_custom_call" | custom-call | flops 200000000 | bytes 4000000 | tf_op jit(solution)/shard_map/pallas_call | solution.py:262
  94.1 14.8 %all_to_all.38.got_ref = f32[32,24,128]{2,1,0:T(8,128)S(1)} all-to-all(f32[32,24,128]{2,1,0:T(8,128)S(1)} %shard_map.69), channel_id=1, replica_groups=mesh['row'=32,'col'=8] {'row'}, dimensions={0} | all-to-all | bytes 786432 | tf_op jit(solution)/shard_map/all_to_all | solution.py:297
  108.9 0.0 copy-done
  108.9 0.0 copy-done.1
  108.9 0.7 shard_map.70
  109.6 14.1 %all_to_all.39 = f32[8,56,128]{2,1,0:T(8,128)S(1)} all-to-all(f32[8,56,128]{2,1,0:T(8,128)S(1)} %broadcast_in_dim.17), channel_id=1, replica_groups=mesh['row'=32,'col'=8] {'col'}, dimensions={0} | all-to-all | bytes 458752 | tf_op jit(solution)/shard_map/all_to_all | solution.py:293
  123.8 24.5 %shard_map.71 = (f32[8,8,128]{2,1,0:T(8,128)S(1)}, f32[32,8,128]{2,1,0:T(8,128)S(1)}) custom-call(f32[448,128]{1,0:T(8,128)S(1)} %bitcast.16, f32[1792,128]{1,0:T(8,128)S(1)} %bitcast.12, f32[448,128]{1,0:T(8,128)S(1)} %bitcast.15, f32[448,1792]{1,0:T(8,128)S(1)} %get-tuple-element.15.f5_ref, f32[448,1792]{1,0:T(8,128)S(1)} %get-tuple-element.16.g7_ref, ...), custom_call_target="tpu_custom_call" | custom-call | flops 300000000 | bytes 4000000 | tf_op jit(solution)/shard_map/pallas_call | solution.py:276
  148.3 12.3 %all_to_all.40.rgot_ref = f32[8,8,128]{2,1,0:T(8,128)S(1)} all-to-all(f32[8,8,128]{2,1,0:T(8,128)S(1)} %get-tuple-element.18), channel_id=1, replica_groups=mesh['row'=32,'col'=8] {'col'}, dimensions={0} | all-to-all | bytes 65536 | tf_op jit(solution)/shard_map/all_to_all | solution.py:297
  160.5 11.1 %all_to_all.41.cgot_ref = f32[32,8,128]{2,1,0:T(8,128)S(1)} all-to-all(f32[32,8,128]{2,1,0:T(8,128)S(1)} %get-tuple-element.19), channel_id=1, replica_groups=mesh['row'=32,'col'=8] {'row'}, dimensions={0} | all-to-all | bytes 262144 | tf_op jit(solution)/shard_map/all_to_all | solution.py:297
  171.6 0.6 shard_map.72
  (4 shorter events, 0.1 us)
Async XLA Ops:
  0.6 43.1 %copy-start.2 = (s32[8,32]{1,0:T(8,128)S(1)}, s32[8,32]{1,0:T(8,128)}, u32[]{:S(2)}) copy-start(s32[8,32]{1,0:T(8,128)} %mask_ref.1) | copy-start | bytes 3076
  90.6 18.3 %copy-start = (f32[3,16,56]{2,1,0:T(8,128)S(1)}, f32[3,16,56]{2,1,0:T(8,128)}, u32[]{:S(2)}) copy-start(f32[3,16,56]{2,1,0:T(8,128)} %param.7) | copy-start | bytes 32260
  90.6 18.3 %copy-start.1 = (f32[56]{0:T(128)S(1)}, f32[56]{0:T(128)}, u32[]{:S(2)}) copy-start(f32[56]{0:T(128)} %param.6) | copy-start | bytes 676

commit v2 on v1

v2 whole, which is shorter than its diff:
```python
import jax
import jax.numpy as jnp
from jax import lax
from jax.experimental import pallas as pl
from jax.experimental.pallas import tpu as pltpu
from jax.sharding import PartitionSpec as P

THOLE_DAMPING = 0.39
HIGHEST = lax.Precision.HIGHEST
F32 = jnp.float32
BF16 = jnp.bfloat16

BEAD = 56
NROW = 32
NCOL = 8
RB = NCOL * BEAD
CB = NROW * BEAD
LANE = 128
GEO = 48
PAIRS = ((0, 0), (1, 1), (2, 2), (0, 1), (0, 2), (1, 2))
VMEM_SPEC = pl.BlockSpec(memory_space=pltpu.VMEM)


def dot_f32(a, b, dims, precision=None):
    return lax.dot_general(a, b, (dims, ((), ())), precision=precision, preferred_element_type=F32)


def hi_lo(x):
    hi = x.astype(BF16).astype(F32)
    return hi, x - hi


def lane_ids(shape):
    return lax.broadcasted_iota(jnp.int32, shape, 1)


def vector_lanes(x):
    return jnp.where(lane_ids(x.shape) < GEO, x, 0.0)


def arranged(u, a, b):
    group = (lane_ids(u.shape) % 64) // 16
    if a == b:
        return jnp.where(group == a, u, 0.0)
    step = 16 * (b - a)
    down = pltpu.roll(u, LANE - step, 1)
    up = pltpu.roll(u, step, 1)
    return jnp.where(group == a, down, jnp.where(group == b, up, 0.0))


def unpack(got_ref, out_ref, blocks):
    for j in range(blocks):
        piece = got_ref[j]
        out_ref[j * BEAD : j * BEAD + 32, :] = piece
        out_ref[j * BEAD + 32 : (j + 1) * BEAD, :] = pltpu.roll(piece[0:24], 64, 1)


def prep_kernel(seeds_ref, dip_ref, pos_ref, pol_ref, v_ref, mu_ref):
    pol = pol_ref[...]
    row = lax.broadcasted_iota(jnp.int32, (16, BEAD), 0)
    geo = jnp.where(row == 3, lax.rsqrt(pol), jnp.where(row == 4, pol, 0.0))
    for i in range(3):
        geo = jnp.where(row == i, pos_ref[i : i + 1, :], geo)
    both = jnp.concatenate([pol * seeds_ref[...], geo, dip_ref[...], geo], axis=0)
    both = jnp.concatenate([both, jnp.zeros((LANE, LANE - BEAD), F32)], axis=1)
    turned = both.T
    swapped = pltpu.roll(turned, 64, 1)
    left = lane_ids((32, LANE)) < 64
    v_ref[...] = jnp.where(left, turned[0:32], swapped[32:64])
    mu_ref[...] = jnp.where(left, swapped[0:32], turned[32:64])


def column_kernel(got_ref, mask_ref, w_ref, xc_ref, m_ref, g_ref):
    unpack(got_ref, g_ref, NROW)
    pick = (lane_ids((8, LANE)) == GEO + lax.broadcasted_iota(jnp.int32, (8, LANE), 0)).astype(F32)
    for k in range(CB // 256):
        rows = pl.ds(k * 256, 256)
        g = g_ref[rows, :]
        xc_ref[:, rows] = dot_f32(pick, g, ((1,), (1,)), HIGHEST)
        hi, lo = hi_lo(vector_lanes(g))
        u = hi + pltpu.roll(lo, 64, 1)
        for n, (a, b) in enumerate(PAIRS):
            w_ref[n, rows, :] = arranged(u, a, b).astype(BF16)
    block = lax.broadcasted_iota(jnp.int32, (NROW, CB), 1) // BEAD
    owner = lax.broadcasted_iota(jnp.int32, (NROW, CB), 0)
    chosen = (block == owner).astype(BF16)
    keep_all = dot_f32(mask_ref[...].astype(F32).astype(BF16), chosen, ((1,), (0,)))
    for k in range(NCOL):
        m_ref[k] = jnp.broadcast_to(keep_all[k : k + 1], (8, CB))


def moment_kernel(got_ref, l_ref, g_ref):
    unpack(got_ref, g_ref, NCOL)
    hi, lo = hi_lo(vector_lanes(g_ref[...]))
    hi = hi + pltpu.roll(hi, 64, 1)
    lo = lo + pltpu.roll(lo, 64, 1)
    for n, (p, q) in enumerate(PAIRS):
        scale = 2.0 if p == q else 1.0
        l_ref[n, :, 0:LANE] = (arranged(hi, p, q) * scale).astype(BF16)
        l_ref[n, :, LANE:] = (arranged(lo, p, q) * scale).astype(BF16)


def build_kernel(
    got_ref, w_ref, xc_ref, m_ref, t_ref, f5_ref, g7_ref, xb_ref, out_ref, g_ref, y_ref
):
    unpack(got_ref, g_ref, NCOL)
    for i in range(4):
        spread = jnp.broadcast_to(g_ref[:, GEO + i : GEO + i + 1], (RB, LANE))
        xb_ref[i] = spread * THOLE_DAMPING if i == 3 else spread

    def row_chunk(q, carry):
        r0 = pl.multiple_of(q * 16, 16)
        rows = pl.ds(r0, 16)
        xr, yr, zr, sr = (xb_ref[i, rows, :] for i in range(4))
        first = (2 * q) // 7
        second = (2 * q + 1) // 7
        for k in range(CB // LANE):
            cols = pl.ds(k * LANE, LANE)
            xc, yc, zc, sc = (jnp.broadcast_to(xc_ref[i : i + 1, cols], (16, LANE)) for i in range(4))
            keep = jnp.concatenate([m_ref[first, :, cols], m_ref[second, :, cols]], axis=0)
            dx, dy, dz = xr - xc, yr - yc, zr - zc
            r2 = dx * dx + dy * dy + dz * dz
            inv = lax.rsqrt(jnp.maximum(r2, 1e-12)) * keep
            v = (r2 * (r2 * inv)) * (sr * sc)
            e = jnp.exp(-v)
            ve = v * e
            one = 1.0 - e
            inv2 = inv * inv
            inv3 = inv2 * inv
            f3 = one * inv3
            inv5 = inv3 * inv2
            f5 = ((one - ve) * 3.0) * inv5
            g7 = inv2 * ((v * ve) * inv5 * 9.0 - 5.0 * f5)
            f5_ref[rows, cols] = f5
            g7_ref[rows, cols] = g7
            fx, fy, fz = f5 * dx, f5 * dy, f5 * dz
            parts = (fx * dx - f3, fy * dy - f3, fz * dz - f3, fx * dy, fx * dz, fy * dz)
            for n, t in enumerate(parts):
                hi = t.astype(BF16)
                t_ref[n, rows, cols] = hi
                t_ref[6 + n, rows, cols] = (t - hi.astype(F32)).astype(BF16)
        return carry

    lax.fori_loop(0, RB // 16, row_chunk, 0)
    total = dot_f32(t_ref[0], w_ref[0], ((1,), (0,)))
    for n in range(1, 12):
        total += dot_f32(t_ref[n], w_ref[n % 6], ((1,), (0,)))
    y_ref[...] = total + pltpu.roll(total, 64, 1)
    left = lane_ids((24, LANE)) < 64
    for k in range(NCOL):
        at = k * BEAD
        out_ref[k, 0:24, :] = jnp.where(left, y_ref[at : at + 24, :], y_ref[at + 32 : at + 56, :])
        out_ref[k, 24:32, :] = y_ref[at + 24 : at + 32, :]


def first_own_kernel(got_ref, v_ref, out_ref):
    y = got_ref[0]
    for k in range(1, NCOL):
        y = y + got_ref[k]
    v = v_ref[...]
    lanes = lane_ids((32, LANE))
    pol = jnp.where(
        lanes < 64,
        jnp.broadcast_to(v[:, GEO + 4 : GEO + 5], (32, LANE)),
        jnp.broadcast_to(v[:, 64 + GEO + 4 : 64 + GEO + 5], (32, LANE)),
    )
    out_ref[...] = jnp.where(lanes % 64 < GEO, v + pol * y, 0.0)


def second_kernel(got_ref, t_ref, out_ref, g_ref, w_ref, y_ref):
    unpack(got_ref, g_ref, NCOL)
    hi, lo = hi_lo(vector_lanes(g_ref[...]))
    ut = (hi + pltpu.roll(lo, 64, 1)).T
    group = (lax.broadcasted_iota(jnp.int32, (LANE, RB), 0) % 64) // 16
    for n, (a, b) in enumerate(PAIRS):
        if a == b:
            w = jnp.where(group == a, ut, 0.0)
        else:
            step = 16 * (b - a)
            down = jnp.concatenate([ut[step:], ut[:step]], axis=0)
            up = jnp.concatenate([ut[LANE - step :], ut[: LANE - step]], axis=0)
            w = jnp.where(group == a, down, jnp.where(group == b, up, 0.0))
        w_ref[n] = w.astype(BF16)
    for k in range(7):
        cols = pl.ds(k * 256, 256)
        total = jnp.zeros((LANE, 256), F32)
        for n in range(12):
            total += dot_f32(w_ref[n % 6], t_ref[n, :, cols], ((1,), (0,)))
        y_ref[:, cols] = total[0:48] + total[64:112]
    for j in range(NROW):
        out_ref[j, :, 0:BEAD] = y_ref[0:24, j * BEAD : (j + 1) * BEAD]
        out_ref[j, :, 64 : 64 + BEAD] = y_ref[24:48, j * BEAD : (j + 1) * BEAD]


def second_own_kernel(got_ref, seeds_ref, pol_ref, field_ref, next_ref):
    y = got_ref[0]
    for k in range(1, NROW):
        y = y + got_ref[k]
    y = jnp.concatenate([y, pltpu.roll(y, 64, 1)], axis=0)
    field = seeds_ref[...] + y[:, 0:BEAD]
    field_ref[...] = field
    vec = pol_ref[...] * field
    vec = jnp.concatenate([vec, jnp.zeros((48, LANE - BEAD), F32)], axis=1)
    turned = jnp.concatenate([vec, jnp.zeros((LANE - 48, LANE), F32)], axis=0).T
    left = lane_ids((32, LANE)) < 64
    next_ref[...] = jnp.where(left, turned[0:32], pltpu.roll(turned[32:64], 64, 1))


def gradient_kernel(
    got_ref, l_ref, xb_ref, f5_ref, g7_ref, xc_ref, or_ref, oc_ref, g_ref, m_ref, h_ref, racc_ref, cacc_ref
):
    unpack(got_ref, g_ref, NROW)
    for k in range(CB // 256):
        rows = pl.ds(k * 256, 256)
        hi, lo = hi_lo(vector_lanes(g_ref[rows, :]))
        u = (hi + pltpu.roll(lo, 64, 1)).astype(BF16)
        m_ref[rows, 0:LANE] = u
        m_ref[rows, LANE:] = u
    racc_ref[...] = jnp.zeros_like(racc_ref)

    def col_chunk(k, carry):
        c0 = pl.multiple_of(k * 256, 256)
        cols = pl.ds(c0, 256)
        for n in range(6):
            h_ref[n] = dot_f32(l_ref[n], m_ref[cols, :], ((1,), (1,)))
        xc, yc, zc = (jnp.broadcast_to(xc_ref[i : i + 1, cols], (8, 256)) for i in range(3))

        def rows_step(t, acc):
            r0 = pl.multiple_of(t * 8, 8)
            rows = pl.ds(r0, 8)
            xr, yr, zr = (jnp.concatenate([xb_ref[i, rows, :]] * 2, axis=1) for i in range(3))
            dx, dy, dz = xr - xc, yr - yc, zr - zc
            hxx, hyy, hzz, hxy, hxz, hyz = (h_ref[n, rows, :] for n in range(6))
            wx = hxx * dx + hxy * dy + hxz * dz
            wy = hxy * dx + hyy * dy + hyz * dz
            wz = hxz * dx + hyz * dy + hzz * dz
            f5 = f5_ref[rows, cols]
            e = g7_ref[rows, cols] * (wx * dx + wy * dy + wz * dz) + f5 * (hxx + hyy + hzz)
            f52 = f5 + f5
            out = []
            for i, (d, w) in enumerate(((dx, wx), (dy, wy), (dz, wz))):
                s = e * d + f52 * w
                racc_ref[i, rows, :] += s[:, 0:LANE] + s[:, LANE:]
                out.append(acc[i] + s)
            return tuple(out)

        zero = jnp.zeros((8, 256), F32)
        acc = lax.fori_loop(0, RB // 8, rows_step, (zero, zero, zero), unroll=4)
        for i in range(3):
            cacc_ref[i : i + 1, cols] = -0.5 * jnp.sum(acc[i], axis=0, keepdims=True)
        return carry

    lax.fori_loop(0, CB // 256, col_chunk, 0)
    ones = jnp.full((8, LANE), 0.5, F32)
    row = lax.broadcasted_iota(jnp.int32, (8, RB), 0)
    total = jnp.zeros((8, RB), F32)
    for i in range(3):
        part = dot_f32(ones, racc_ref[i], ((1,), (1,)), HIGHEST)
        total = jnp.where(row == i, part, total)
    for j in range(NCOL):
        or_ref[j, :, 0:BEAD] = total[:, j * BEAD : (j + 1) * BEAD]
    for j in range(NROW):
        oc_ref[j, :, 0:BEAD] = cacc_ref[:, j * BEAD : (j + 1) * BEAD]


def final_kernel(rgot_ref, cgot_ref, out_ref):
    total = rgot_ref[0]
    for k in range(1, NCOL):
        total = total + rgot_ref[k]
    for k in range(NROW):
        total = total + cgot_ref[k]
    out_ref[...] = total[0:3, 0:BEAD]


def call(kernel, outs, scratch, flops, limit_mib):
    return pl.pallas_call(
        kernel,
        out_shape=[jax.ShapeDtypeStruct(s, t) for s, t in outs],
        out_specs=[VMEM_SPEC] * len(outs),
        scratch_shapes=[pltpu.VMEM(s, t) for s, t in scratch],
        compiler_params=pltpu.CompilerParams(vmem_limit_bytes=limit_mib << 20),
        cost_estimate=pl.CostEstimate(flops=flops, bytes_accessed=1_000_000, transcendentals=0),
    )


def run_prep(seeds, dipoles, positions, pol):
    outs = [((32, LANE), F32)] * 2
    return call(prep_kernel, outs, [], 100_000, 4)(seeds, dipoles, positions, pol)


def run_columns(got, mask):
    outs = [((6, CB, LANE), BF16), ((8, CB), F32), ((NCOL, 8, CB), F32)]
    return call(column_kernel, outs, [((CB, LANE), F32)], 2_000_000, 8)(got, mask)


def run_moments(got):
    return call(moment_kernel, [((6, RB, 2 * LANE), BF16)], [((RB, LANE), F32)], 1_000_000, 4)(got)[0]


def run_build(got, w, xc, m):
    outs = [
        ((12, RB, CB), BF16),
        ((RB, CB), F32),
        ((RB, CB), F32),
        ((4, RB, LANE), F32),
        ((NCOL, 32, LANE), F32),
    ]
    scratch = [((RB, LANE), F32), ((RB, LANE), F32)]
    return call(build_kernel, outs, scratch, 400_000_000, 6)(got, w, xc, m)


def run_first_own(got, v):
    return call(first_own_kernel, [((32, LANE), F32)], [], 100_000, 4)(got, v)[0]


def run_second(got, t):
    scratch = [((RB, LANE), F32), ((6, LANE, RB), BF16), ((48, CB), F32)]
    return call(second_kernel, [((NROW, 24, LANE), F32)], scratch, 200_000_000, 6)(got, t)[0]


def run_second_own(got, seeds, pol):
    outs = [((48, BEAD), F32), ((32, LANE), F32)]
    return call(second_own_kernel, outs, [], 100_000, 4)(got, seeds, pol)


def run_gradient(got, l, xb, f5, g7, xc):
    outs = [((NCOL, 8, LANE), F32), ((NROW, 8, LANE), F32)]
    scratch = [
        ((CB, LANE), F32),
        ((CB, 2 * LANE), BF16),
        ((6, RB, 256), F32),
        ((3, RB, LANE), F32),
        ((8, CB), F32),
    ]
    return call(gradient_kernel, outs, scratch, 300_000_000, 10)(got, l, xb, f5, g7, xc)


def run_final(rgot, cgot):
    return call(final_kernel, [((3, BEAD), F32)], [], 100_000, 4)(rgot, cgot)[0]


def exchange(x, axis):
    return lax.all_to_all(x, axis, 0, 0, tiled=True)


def broadcast_all(x, axis):
    return exchange(jnp.broadcast_to(x[None], (lax.axis_size(axis), *x.shape)), axis)


def local(positions, polarizability, seeds, dipoles, tile_mask):
    seeds = seeds.reshape(48, BEAD)
    pol = polarizability[None, :]
    own_v, own_mu = run_prep(seeds, dipoles.reshape(48, BEAD), positions, pol)
    w, xc, m = run_columns(broadcast_all(own_v, "row"), tile_mask)
    got_mu = broadcast_all(own_mu, "col")
    moments = run_moments(got_mu)
    t, f5, g7, xb, parts = run_build(got_mu, w, xc, m)
    own_next = run_first_own(exchange(parts, "col"), own_v)
    pieces = run_second(broadcast_all(own_next, "col"), t)
    field, own_adjoint = run_second_own(exchange(pieces, "row"), seeds, pol)
    out_r, out_c = run_gradient(broadcast_all(own_adjoint, "row"), moments, xb, f5, g7, xc)
    gradient = run_final(exchange(out_r, "col"), exchange(out_c, "row"))
    return (field.reshape(3, 16, BEAD), gradient)


def solution(mesh):
    in_specs = (
        P(None, ("row", "col")),
        P(("row", "col")),
        P(None, None, ("row", "col")),
        P(None, None, ("row", "col")),
        P("row", "col"),
    )
    out_specs = (P(None, None, ("row", "col")), P(None, ("row", "col")))
    return jax.shard_map(local, mesh=mesh, in_specs=in_specs, out_specs=out_specs, check_vma=False)
```

time: 173 us -> 154 us (0.89)
  blocking collectives: 121 us -> 79.8 us
  Pallas kernels: 46.2 us -> 31.2 us
  starting transfers between devices: 0 us -> 14.3 us
  waiting for transfers between devices: 0 us -> 13.8 us
  local copies, waits for them, and re-layouts: 3.46 us -> 13.2 us
    all_to_all x4 -> x0, blocking collectives: 82.9 us -> none  [broadcast_all(): lax.all_to_all(jnp.broadcast_to(x[None], (n, *x.shape)), axis, 0, 0, tile...]
    all_to_all x3 -> x6, blocking collectives: 38.2 us -> 79.8 us  [exchange(): return lax.all_to_all(x, axis, 0, 0, tiled=True)]
    pallas_call x5 -> x9, Pallas kernels: 46.2 us -> 31.2 us  [the longest x1 13.7 us: run_build(): return call(build_kernel, outs, scratch, 400000000, 6)(got, w, xc, m)]
    all_to_all x0 -> x2, starting transfers between devices: none -> 14.3 us  [exchange(): return lax.all_to_all(x, axis, 0, 0, tiled=True)]
    all_to_all x0 -> x2, waiting for transfers between devices: none -> 13.8 us  [exchange(): return lax.all_to_all(x, axis, 0, 0, tiled=True)]
    unnamed x7 -> x30, local copies, waits for them, and re-layouts: 0.79 us -> 11.7 us
  transfers between devices with their start and end apart: 0 -> 2, of which waited for: 0 -> 2; matrix products, arithmetic and copies ran while one was open for 0% -> 0% of each run, Pallas kernels for 0% -> 1%
where the time goes in v2:
time: 154 us; the launch traced here: 153 us
  blocking collectives  79.8 us (52%)
  Pallas kernels  31.2 us (20%)
  starting transfers between devices  14.3 us (9%)
  waiting for transfers between devices  13.8 us (9%)
  local copies, waits for them, and re-layouts  13.2 us (9%)
    all_to_all x6, blocking collectives, exchange(): return lax.all_to_all(x, axis, 0, 0, tiled=True)  79.8 us
    all_to_all x2, starting transfers between devices, exchange(): return lax.all_to_all(x, axis, 0, 0, tiled=True)  14.3 us
    all_to_all x2, waiting for transfers between devices, exchange(): return lax.all_to_all(x, axis, 0, 0, tiled=True)  13.8 us
    pallas_call x1, Pallas kernels, run_build(): return call(build_kernel, outs, scratch, 400000000, 6)(got, w, xc, m)  13.7 us
    unnamed x30, local copies, waits for them, and re-layouts  11.7 us
    pallas_call x1, Pallas kernels, run_gradient(): call(gradient_kernel, outs, scratch, 300000000, 10)(got, l, xb, f5, g7, xc)  10.7 us
    pallas_call x1, Pallas kernels, run_second(): call(second_kernel, [((NROW, 24, LANE), F32)], scratch, 200000000, 6)  3.37 us
  transfers between devices with their start and end apart: 2, of which 2 were waited for; matrix products, arithmetic and copies ran while one was open for 0% of the time, Pallas kernels for 1%

profile of v2, /device:TPU:1, one launch (start us, length us, event | category | flops | bytes accessed | tf_op | source)
XLA Modules:
  0.0 153.1 jit_solution(15812928499951440970)
XLA Ops:
  0.6 0.0 copy-start.8
  0.6 0.7 copy-done.8
  1.4 0.0 copy-start.10
  1.4 0.7 copy-done.10
  2.1 0.0 copy-start.12
  2.1 0.7 copy-done.12
  2.8 0.0 copy-start.14
  2.8 0.7 copy-done.14
  3.4 0.1 shard_map.68
  3.6 0.1 broadcast_in_dim.12
  3.7 19.0 %all_to_all.40.got_ref = f32[32,32,128]{2,1,0:T(8,128)S(1)} all-to-all(f32[32,32,128]{2,1,0:T(8,128)S(1)} %broadcast_in_dim.12), channel_id=1, replica_groups=mesh['row'=32,'col'=8] {'row'}, dimensions={0} | all-to-all | bytes 1048576 | tf_op jit(solution)/shard_map/all_to_all | solution.py:343
  22.7 0.7 broadcast_in_dim.11
  23.3 10.1 %all-to-all-start = ((f32[8,32,128]{2,1,0:T(8,128)}), f32[8,32,128]{2,1,0:T(8,128)S(1)}, u32[]{:S(2)}, u32[]{:S(2)}) async-start(f32[8,32,128]{2,1,0:T(8,128)} %broadcast_in_dim.11), calls=%async_computation | async-start | bytes 262144 | tf_op jit(solution)/shard_map/all_to_all | solution.py:343
  33.4 0.0 copy-start.11
  33.4 0.7 copy-done.11
  34.1 1.4 shard_map.69
  35.5 0.0 copy-start.6
  35.5 0.8 copy-done.6
  36.3 5.2 %all-to-all-done.got_ref = f32[8,32,128]{2,1,0:T(8,128)S(1)} async-done(((f32[8,32,128]{2,1,0:T(8,128)}), f32[8,32,128]{2,1,0:T(8,128)S(1)}, u32[]{:S(2)}, u32[]{:S(2)}) %all-to-all-start) | async-done | bytes 131104 | tf_op jit(solution)/shard_map/all_to_all | solution.py:343
  41.5 0.0 copy-start.7
  41.5 1.0 copy-done.7
  42.5 13.7 %shard_map.70 = (bf16[12,448,1792]{2,1,0:T(8,128)(2,1)S(1)}, f32[448,1792]{1,0:T(8,128)S(1)}, f32[448,1792]{1,0:T(8,128)S(1)}, f32[4,448,128]{2,1,0:T(8,128)S(1)}, f32[8,32,128]{2,1,0:T(8,128)S(1)}) custom-call(f32[8,32,128]{2,1,0:T(8,128)S(1)} %all-to-all-done.got_ref, bf16[6,1792,128]{2,1,0:T(8,128)(2,1)S(1)} %get-tuple-element.18.w_ref, ...), custom_call_target="tpu_custom_call" | custom-call | flops 400000000 | bytes 1000000 | tf_op jit(solution)/shard_map/pallas_call | solution.py:309
  56.2 0.0 copy-start
  56.2 1.6 %copy-done = f32[448,1792]{1,0:T(8,128)} copy-done((f32[448,1792]{1,0:T(8,128)}, f32[448,1792]{1,0:T(8,128)S(1)}, u32[]{:S(2)}) %copy-start) | copy-done | bytes 3211288
  57.9 0.0 copy-start.4
  57.9 0.9 copy-done.4
  58.8 0.0 copy-start.2
  58.8 11.5 %all_to_all.41.got_ref = f32[8,32,128]{2,1,0:T(8,128)S(1)} all-to-all(f32[8,32,128]{2,1,0:T(8,128)S(1)} %get-tuple-element.21), channel_id=1, replica_groups=mesh['row'=32,'col'=8] {'col'}, dimensions={0} | all-to-all | bytes 262144 | tf_op jit(solution)/shard_map/all_to_all | solution.py:343
  70.3 0.1 shard_map.71
  70.4 12.2 %all_to_all.42.got_ref = f32[8,32,128]{2,1,0:T(8,128)S(1)} all-to-all(f32[8,32,128]{2,1,0:T(8,128)S(1)} %broadcast_in_dim.13), channel_id=1, replica_groups=mesh['row'=32,'col'=8] {'col'}, dimensions={0} | all-to-all | bytes 262144 | tf_op jit(solution)/shard_map/all_to_all | solution.py:343
  82.7 3.4 %shard_map.72 = f32[32,24,128]{2,1,0:T(8,128)S(1)} custom-call(f32[8,32,128]{2,1,0:T(8,128)S(1)} %all_to_all.42.got_ref, bf16[12,448,1792]{2,1,0:T(8,128)(2,1)S(1)} %get-tuple-element.22.t_ref), custom_call_target="tpu_custom_call" | custom-call | flops 200000000 | bytes 1000000 | tf_op jit(solution)/shard_map/pallas_call | solution.py:318
  86.0 0.0 copy-done.2
  86.0 0.0 copy-start.5
  86.1 12.3 %all_to_all.43.got_ref = f32[32,24,128]{2,1,0:T(8,128)S(1)} all-to-all(f32[32,24,128]{2,1,0:T(8,128)S(1)} %shard_map.72), channel_id=1, replica_groups=mesh['row'=32,'col'=8] {'row'}, dimensions={0} | all-to-all | bytes 786432 | tf_op jit(solution)/shard_map/all_to_all | solution.py:343
  98.4 0.0 copy-done.9
  98.4 0.0 copy-done.13
  98.4 0.7 shard_map.73
  99.1 0.8 broadcast_in_dim.14
  99.9 4.2 %all-to-all-start.5 = ((f32[32,32,128]{2,1,0:T(8,128)}), f32[32,32,128]{2,1,0:T(8,128)S(1)}, u32[]{:S(2)}, u32[]{:S(2)}) async-start(f32[32,32,128]{2,1,0:T(8,128)} %broadcast_in_dim.14), calls=%async_computation.5 | async-start | bytes 1048576 | tf_op jit(solution)/shard_map/all_to_all | solution.py:343
  104.1 0.5 shard_map.74.l_ref
  104.7 8.5 %all-to-all-done.5.got_ref = f32[32,32,128]{2,1,0:T(8,128)S(1)} async-done(((f32[32,32,128]{2,1,0:T(8,128)}), f32[32,32,128]{2,1,0:T(8,128)S(1)}, u32[]{:S(2)}, u32[]{:S(2)}) %all-to-all-start.5) | async-done | bytes 524320 | tf_op jit(solution)/shard_map/all_to_all | solution.py:343
  113.2 0.0 copy-done.5
  113.2 1.9 %copy-done.1 = f32[448,1792]{1,0:T(8,128)S(1)} copy-done((f32[448,1792]{1,0:T(8,128)S(1)}, f32[448,1792]{1,0:T(8,128)}, u32[]{:S(2)}) %copy-start.1) | copy-done | bytes 3211288
  115.1 1.9 %copy-done.3 = f32[448,1792]{1,0:T(8,128)S(1)} copy-done((f32[448,1792]{1,0:T(8,128)S(1)}, f32[448,1792]{1,0:T(8,128)}, u32[]{:S(2)}) %copy-start.3) | copy-done | bytes 3211288
  117.0 10.7 %shard_map.75 = (f32[8,8,128]{2,1,0:T(8,128)S(1)}, f32[32,8,128]{2,1,0:T(8,128)S(1)}) custom-call(f32[32,32,128]{2,1,0:T(8,128)S(1)} %all-to-all-done.5.got_ref, bf16[6,448,256]{2,1,0:T(8,128)(2,1)S(1)} %shard_map.74.l_ref, f32[4,448,128]{2,1,0:T(8,128)S(1)} %copy-done.5, f32[448,1792]{1,0:T(8,128)S(1)} %copy-done.1, f32[448,1792]{1,0:T(8,128)S(1)} %copy-done.3, ...), custom_call_target="tpu_custom_call" | custom-call | flops 300000000 | bytes 1000000 | tf_op jit(solution)/shard_map/pallas_call | solution.py:335
  127.7 13.9 %all_to_all.44.rgot_ref = f32[8,8,128]{2,1,0:T(8,128)S(1)} all-to-all(f32[8,8,128]{2,1,0:T(8,128)S(1)} %get-tuple-element.28), channel_id=1, replica_groups=mesh['row'=32,'col'=8] {'col'}, dimensions={0} | all-to-all | bytes 65536 | tf_op jit(solution)/shard_map/all_to_all | solution.py:343
  141.6 10.8 %all_to_all.45.cgot_ref = f32[32,8,128]{2,1,0:T(8,128)S(1)} all-to-all(f32[32,8,128]{2,1,0:T(8,128)S(1)} %get-tuple-element.29), channel_id=1, replica_groups=mesh['row'=32,'col'=8] {'row'}, dimensions={0} | all-to-all | bytes 262144 | tf_op jit(solution)/shard_map/all_to_all | solution.py:343
  152.4 0.6 shard_map.76
  (5 shorter events, 0.0 us)
Async XLA Ops:
  0.6 0.7 copy-start.8
  1.4 0.7 copy-start.10
  2.1 0.7 copy-start.12
  2.8 0.7 copy-start.14
  23.3 18.2 %all-to-all-start = ((f32[8,32,128]{2,1,0:T(8,128)}), f32[8,32,128]{2,1,0:T(8,128)S(1)}, u32[]{:S(2)}, u32[]{:S(2)}) async-start(f32[8,32,128]{2,1,0:T(8,128)} %broadcast_in_dim.11), calls=%async_computation | async-start | bytes 262144 | tf_op jit(solution)/shard_map/all_to_all | solution.py:343
  33.4 0.7 copy-start.11
  35.5 0.8 copy-start.6
  41.5 1.0 copy-start.7
  56.2 1.7 %copy-start = (f32[448,1792]{1,0:T(8,128)}, f32[448,1792]{1,0:T(8,128)S(1)}, u32[]{:S(2)}) copy-start(f32[448,1792]{1,0:T(8,128)S(1)} %get-tuple-element.26.f5_ref) | copy-start | bytes 9633796
  57.9 0.9 copy-start.4
  58.8 27.2 %copy-start.2 = (f32[448,1792]{1,0:T(8,128)}, f32[448,1792]{1,0:T(8,128)S(1)}, u32[]{:S(2)}) copy-start(f32[448,1792]{1,0:T(8,128)S(1)} %get-tuple-element.27.g7_ref) | copy-start | bytes 9633796
  82.7 15.7 %copy-start.9 = (f32[3,16,56]{2,1,0:T(8,128)S(1)}, f32[3,16,56]{2,1,0:T(8,128)}, u32[]{:S(2)}) copy-start(f32[3,16,56]{2,1,0:T(8,128)} %param.7) | copy-start | bytes 32260
  82.7 15.7 %copy-start.13 = (f32[56]{0:T(128)S(1)}, f32[56]{0:T(128)}, u32[]{:S(2)}) copy-start(f32[56]{0:T(128)} %param.6) | copy-start | bytes 676
  86.0 27.2 %copy-start.5 = (f32[4,448,128]{2,1,0:T(8,128)S(1)}, f32[4,448,128]{2,1,0:T(8,128)}, u32[]{:S(2)}) copy-start(f32[4,448,128]{2,1,0:T(8,128)} %copy-done.4) | copy-start | bytes 2752516
  99.9 13.3 %all-to-all-start.5 = ((f32[32,32,128]{2,1,0:T(8,128)}), f32[32,32,128]{2,1,0:T(8,128)S(1)}, u32[]{:S(2)}, u32[]{:S(2)}) async-start(f32[32,32,128]{2,1,0:T(8,128)} %broadcast_in_dim.14), calls=%async_computation.5 | async-start | bytes 1048576 | tf_op jit(solution)/shard_map/all_to_all | solution.py:343
  113.2 1.9 %copy-start.1 = (f32[448,1792]{1,0:T(8,128)S(1)}, f32[448,1792]{1,0:T(8,128)}, u32[]{:S(2)}) copy-start(f32[448,1792]{1,0:T(8,128)} %copy-done) | copy-start | bytes 9633796
  115.1 1.9 %copy-start.3 = (f32[448,1792]{1,0:T(8,128)S(1)}, f32[448,1792]{1,0:T(8,128)}, u32[]{:S(2)}) copy-start(f32[448,1792]{1,0:T(8,128)} %copy-done.2) | copy-start | bytes 9633796

commit v3 on v2

--- a/solution.py
+++ b/solution.py
@@ -55,28 +55,33 @@
         out_ref[j * BEAD + 32 : (j + 1) * BEAD, :] = pltpu.roll(piece[0:24], 64, 1)
 
 
-def prep_kernel(seeds_ref, dip_ref, pos_ref, pol_ref, v_ref, mu_ref):
-    pol = pol_ref[...]
+def prep_kernel(x_ref, own_ref, v_ref, mu_ref, mask_ref):
+    pol = x_ref[99:100, :]
     row = lax.broadcasted_iota(jnp.int32, (16, BEAD), 0)
     geo = jnp.where(row == 3, lax.rsqrt(pol), jnp.where(row == 4, pol, 0.0))
     for i in range(3):
-        geo = jnp.where(row == i, pos_ref[i : i + 1, :], geo)
-    both = jnp.concatenate([pol * seeds_ref[...], geo, dip_ref[...], geo], axis=0)
+        geo = jnp.where(row == i, x_ref[96 + i : 97 + i, :], geo)
+    both = jnp.concatenate([pol * x_ref[0:48, :], geo, x_ref[48:96, :], geo], axis=0)
     both = jnp.concatenate([both, jnp.zeros((LANE, LANE - BEAD), F32)], axis=1)
     turned = both.T
     swapped = pltpu.roll(turned, 64, 1)
     left = lane_ids((32, LANE)) < 64
-    v_ref[...] = jnp.where(left, turned[0:32], swapped[32:64])
-    mu_ref[...] = jnp.where(left, swapped[0:32], turned[32:64])
-
-
-def column_kernel(got_ref, mask_ref, w_ref, xc_ref, m_ref, g_ref):
+    own = jnp.where(left, turned[0:32], swapped[32:64])
+    own_ref[...] = own
+    for k in range(NROW):
+        v_ref[k] = own
+    own = jnp.where(left, swapped[0:32], turned[32:64])
+    for k in range(NCOL):
+        mu_ref[k] = own
+    mask_ref[...] = x_ref[104:112, 0:NROW]
+
+
+def prepare_columns(got_ref, mask_ref, w_ref, xc_ref, m_ref, g_ref):
     unpack(got_ref, g_ref, NROW)
-    pick = (lane_ids((8, LANE)) == GEO + lax.broadcasted_iota(jnp.int32, (8, LANE), 0)).astype(F32)
     for k in range(CB // 256):
         rows = pl.ds(k * 256, 256)
         g = g_ref[rows, :]
-        xc_ref[:, rows] = dot_f32(pick, g, ((1,), (1,)), HIGHEST)
+        xc_ref[:, rows] = g.T[GEO : GEO + 8]
         hi, lo = hi_lo(vector_lanes(g))
         u = hi + pltpu.roll(lo, 64, 1)
         for n, (a, b) in enumerate(PAIRS):
@@ -84,13 +89,12 @@
     block = lax.broadcasted_iota(jnp.int32, (NROW, CB), 1) // BEAD
     owner = lax.broadcasted_iota(jnp.int32, (NROW, CB), 0)
     chosen = (block == owner).astype(BF16)
-    keep_all = dot_f32(mask_ref[...].astype(F32).astype(BF16), chosen, ((1,), (0,)))
+    keep_all = dot_f32(mask_ref[...].astype(BF16), chosen, ((1,), (0,)))
     for k in range(NCOL):
         m_ref[k] = jnp.broadcast_to(keep_all[k : k + 1], (8, CB))
 
 
-def moment_kernel(got_ref, l_ref, g_ref):
-    unpack(got_ref, g_ref, NCOL)
+def prepare_moments(l_ref, g_ref):
     hi, lo = hi_lo(vector_lanes(g_ref[...]))
     hi = hi + pltpu.roll(hi, 64, 1)
     lo = lo + pltpu.roll(lo, 64, 1)
@@ -101,9 +105,25 @@
 
 
 def build_kernel(
-    got_ref, w_ref, xc_ref, m_ref, t_ref, f5_ref, g7_ref, xb_ref, out_ref, g_ref, y_ref
+    gotv_ref,
+    gotm_ref,
+    mask_ref,
+    t_ref,
+    f5_ref,
+    g7_ref,
+    xb_ref,
+    xc_ref,
+    l_ref,
+    out_ref,
+    gc_ref,
+    g_ref,
+    y_ref,
+    w_ref,
+    m_ref,
 ):
-    unpack(got_ref, g_ref, NCOL)
+    prepare_columns(gotv_ref, mask_ref, w_ref, xc_ref, m_ref, gc_ref)
+    unpack(gotm_ref, g_ref, NCOL)
+    prepare_moments(l_ref, g_ref)
     for i in range(4):
         spread = jnp.broadcast_to(g_ref[:, GEO + i : GEO + i + 1], (RB, LANE))
         xb_ref[i] = spread * THOLE_DAMPING if i == 3 else spread
@@ -164,29 +184,32 @@
         jnp.broadcast_to(v[:, GEO + 4 : GEO + 5], (32, LANE)),
         jnp.broadcast_to(v[:, 64 + GEO + 4 : 64 + GEO + 5], (32, LANE)),
     )
-    out_ref[...] = jnp.where(lanes % 64 < GEO, v + pol * y, 0.0)
+    own = jnp.where(lanes % 64 < GEO, v + pol * y, 0.0)
+    for k in range(NCOL):
+        out_ref[k] = own
 
 
 def second_kernel(got_ref, t_ref, out_ref, g_ref, w_ref, y_ref):
     unpack(got_ref, g_ref, NCOL)
     hi, lo = hi_lo(vector_lanes(g_ref[...]))
     ut = (hi + pltpu.roll(lo, 64, 1)).T
-    group = (lax.broadcasted_iota(jnp.int32, (LANE, RB), 0) % 64) // 16
+    ut = jnp.concatenate([ut[0:48], ut[64:112]], axis=0)
+    group = (lax.broadcasted_iota(jnp.int32, (96, RB), 0) % 48) // 16
     for n, (a, b) in enumerate(PAIRS):
         if a == b:
             w = jnp.where(group == a, ut, 0.0)
         else:
             step = 16 * (b - a)
             down = jnp.concatenate([ut[step:], ut[:step]], axis=0)
-            up = jnp.concatenate([ut[LANE - step :], ut[: LANE - step]], axis=0)
+            up = jnp.concatenate([ut[96 - step :], ut[: 96 - step]], axis=0)
             w = jnp.where(group == a, down, jnp.where(group == b, up, 0.0))
         w_ref[n] = w.astype(BF16)
     for k in range(7):
         cols = pl.ds(k * 256, 256)
-        total = jnp.zeros((LANE, 256), F32)
+        total = jnp.zeros((96, 256), F32)
         for n in range(12):
             total += dot_f32(w_ref[n % 6], t_ref[n, :, cols], ((1,), (0,)))
-        y_ref[:, cols] = total[0:48] + total[64:112]
+        y_ref[:, cols] = total[0:48] + total[48:96]
     for j in range(NROW):
         out_ref[j, :, 0:BEAD] = y_ref[0:24, j * BEAD : (j + 1) * BEAD]
         out_ref[j, :, 64 : 64 + BEAD] = y_ref[24:48, j * BEAD : (j + 1) * BEAD]
@@ -203,7 +226,9 @@
     vec = jnp.concatenate([vec, jnp.zeros((48, LANE - BEAD), F32)], axis=1)
     turned = jnp.concatenate([vec, jnp.zeros((LANE - 48, LANE), F32)], axis=0).T
     left = lane_ids((32, LANE)) < 64
-    next_ref[...] = jnp.where(left, turned[0:32], pltpu.roll(turned[32:64], 64, 1))
+    own = jnp.where(left, turned[0:32], pltpu.roll(turned[32:64], 64, 1))
+    for k in range(NROW):
+        next_ref[k] = own
 
 
 def gradient_kernel(
@@ -283,43 +308,42 @@
     )
 
 
-def run_prep(seeds, dipoles, positions, pol):
-    outs = [((32, LANE), F32)] * 2
-    return call(prep_kernel, outs, [], 100_000, 4)(seeds, dipoles, positions, pol)
-
-
-def run_columns(got, mask):
-    outs = [((6, CB, LANE), BF16), ((8, CB), F32), ((NCOL, 8, CB), F32)]
-    return call(column_kernel, outs, [((CB, LANE), F32)], 2_000_000, 8)(got, mask)
-
-
-def run_moments(got):
-    return call(moment_kernel, [((6, RB, 2 * LANE), BF16)], [((RB, LANE), F32)], 1_000_000, 4)(got)[0]
-
-
-def run_build(got, w, xc, m):
+def run_prep(x):
+    outs = [((32, LANE), F32), ((NROW, 32, LANE), F32), ((NCOL, 32, LANE), F32), ((NCOL, NROW), F32)]
+    return call(prep_kernel, outs, [], 100_000, 4)(x)
+
+
+def run_build(gotv, gotm, mask):
     outs = [
         ((12, RB, CB), BF16),
         ((RB, CB), F32),
         ((RB, CB), F32),
         ((4, RB, LANE), F32),
+        ((8, CB), F32),
+        ((6, RB, 2 * LANE), BF16),
         ((NCOL, 32, LANE), F32),
     ]
-    scratch = [((RB, LANE), F32), ((RB, LANE), F32)]
-    return call(build_kernel, outs, scratch, 400_000_000, 6)(got, w, xc, m)
+    scratch = [
+        ((CB, LANE), F32),
+        ((RB, LANE), F32),
+        ((RB, LANE), F32),
+        ((6, CB, LANE), BF16),
+        ((NCOL, 8, CB), F32),
+    ]
+    return call(build_kernel, outs, scratch, 400_000_000, 8)(gotv, gotm, mask)
 
 
 def run_first_own(got, v):
-    return call(first_own_kernel, [((32, LANE), F32)], [], 100_000, 4)(got, v)[0]
+    return call(first_own_kernel, [((NCOL, 32, LANE), F32)], [], 100_000, 4)(got, v)[0]
 
 
 def run_second(got, t):
-    scratch = [((RB, LANE), F32), ((6, LANE, RB), BF16), ((48, CB), F32)]
+    scratch = [((RB, LANE), F32), ((6, 96, RB), BF16), ((48, CB), F32)]
     return call(second_kernel, [((NROW, 24, LANE), F32)], scratch, 200_000_000, 6)(got, t)[0]
 
 
 def run_second_own(got, seeds, pol):
-    outs = [((48, BEAD), F32), ((32, LANE), F32)]
+    outs = [((48, BEAD), F32), ((NROW, 32, LANE), F32)]
     return call(second_own_kernel, outs, [], 100_000, 4)(got, seeds, pol)
 
 
@@ -332,7 +356,7 @@
         ((3, RB, LANE), F32),
         ((8, CB), F32),
     ]
-    return call(gradient_kernel, outs, scratch, 300_000_000, 10)(got, l, xb, f5, g7, xc)
+    return call(gradient_kernel, outs, scratch, 300_000_000, 12)(got, l, xb, f5, g7, xc)
 
 
 def run_final(rgot, cgot):
@@ -341,24 +365,23 @@
 
 def exchange(x, axis):
     return lax.all_to_all(x, axis, 0, 0, tiled=True)
-
-
-def broadcast_all(x, axis):
-    return exchange(jnp.broadcast_to(x[None], (lax.axis_size(axis), *x.shape)), axis)
 
 
 def local(positions, polarizability, seeds, dipoles, tile_mask):
     seeds = seeds.reshape(48, BEAD)
     pol = polarizability[None, :]
-    own_v, own_mu = run_prep(seeds, dipoles.reshape(48, BEAD), positions, pol)
-    w, xc, m = run_columns(broadcast_all(own_v, "row"), tile_mask)
-    got_mu = broadcast_all(own_mu, "col")
-    moments = run_moments(got_mu)
-    t, f5, g7, xb, parts = run_build(got_mu, w, xc, m)
+    mask = jnp.pad(tile_mask.astype(F32), ((0, 0), (0, BEAD - NROW)))
+    blank = jnp.zeros((4, BEAD), F32)
+    own_v, all_v, all_mu, mask = run_prep(
+        jnp.concatenate([seeds, dipoles.reshape(48, BEAD), positions, pol, blank, mask], axis=0)
+    )
+    got_v = exchange(all_v, "row")
+    got_mu = exchange(all_mu, "col")
+    t, f5, g7, xb, xc, moments, parts = run_build(got_v, got_mu, mask)
     own_next = run_first_own(exchange(parts, "col"), own_v)
-    pieces = run_second(broadcast_all(own_next, "col"), t)
+    pieces = run_second(exchange(own_next, "col"), t)
     field, own_adjoint = run_second_own(exchange(pieces, "row"), seeds, pol)
-    out_r, out_c = run_gradient(broadcast_all(own_adjoint, "row"), moments, xb, f5, g7, xc)
+    out_r, out_c = run_gradient(exchange(own_adjoint, "row"), moments, xb, f5, g7, xc)
     gradient = run_final(exchange(out_r, "col"), exchange(out_c, "row"))
     return (field.reshape(3, 16, BEAD), gradient)
 

time: 154 us -> 145 us (0.942)
  blocking collectives: 79.8 us -> 110 us
  starting transfers between devices: 14.3 us -> 0 us
  waiting for transfers between devices: 13.8 us -> 0 us
  local copies, waits for them, and re-layouts: 13.2 us -> 2.19 us
    all_to_all x6 -> x8, blocking collectives: 79.8 us -> 110 us  [exchange(): return lax.all_to_all(x, axis, 0, 0, tiled=True)]
    all_to_all x2 -> x0, starting transfers between devices: 14.3 us -> none  [exchange(): return lax.all_to_all(x, axis, 0, 0, tiled=True)]
    all_to_all x2 -> x0, waiting for transfers between devices: 13.8 us -> none  [exchange(): return lax.all_to_all(x, axis, 0, 0, tiled=True)]
    unnamed x30 -> x4, local copies, waits for them, and re-layouts: 11.7 us -> 0.01 us
    concatenate x0 -> x1, local copies, waits for them, and re-layouts: none -> 2.18 us  [local(): jnp.concatenate([seeds, dipoles.reshape(48, BEAD), positions, pol, blank,...]
    broadcast_in_dim x4 -> x1, local copies, waits for them, and re-layouts: 1.56 us -> 0.01 us  [local(): blank = jnp.zeros((4, BEAD), F32)]
    pallas_call x6 -> x4, Pallas kernels: 26.5 us -> 26.6 us  [the longest x1 15.6 us: run_build(): return call(build_kernel, outs, scratch, 400000000, 8)(gotv, gotm, mask)]
  transfers between devices with their start and end apart: 2 -> 0, of which waited for: 2 -> 0; matrix products, arithmetic and copies ran while one was open for 0% -> 0% of each run, Pallas kernels for 1% -> 0%
where the time goes in v3:
time: 145 us; the launch traced here: 144 us
  blocking collectives  110 us (76%)
  Pallas kernels  31.1 us (21%)
  local copies, waits for them, and re-layouts  2.19 us (2%)
    all_to_all x8, blocking collectives, exchange(): return lax.all_to_all(x, axis, 0, 0, tiled=True)  110 us
    pallas_call x1, Pallas kernels, run_build(): return call(build_kernel, outs, scratch, 400000000, 8)(gotv, gotm, mask)  15.6 us
    pallas_call x1, Pallas kernels, run_gradient(): call(gradient_kernel, outs, scratch, 300000000, 12)(got, l, xb, f5, g7, xc)  10.7 us
    pallas_call x1, Pallas kernels, run_second(): call(second_kernel, [((NROW, 24, LANE), F32)], scratch, 200000000, 6)  3.09 us

profile of v3, /device:TPU:1, one launch (start us, length us, event | category | flops | bytes accessed | tf_op | source)
XLA Modules:
  0.0 144.4 jit_solution(7759168326953891925)
XLA Ops:
  0.6 0.7 convert_element_type.5
  1.3 2.2 %concatenate.3.x_ref = f32[112,56]{1,0:T(8,128)S(1)} concatenate(f32[48,56]{1,0:T(8,128)} %bitcast.4, f32[48,56]{1,0:T(8,128)} %bitcast.8, f32[3,56]{1,0:T(4,128)} %param.5, f32[1,56]{1,0:T(1,128)} %bitcast.6, f32[4,56]{1,0:T(4,128)S(1)} %broadcast_in_dim.7, f32[8,56]{1,0:T(8,128)S(1)} %pad.4), dimensions={0} | concatenate | bytes 50176 | tf_op jit(solution)/shard_map/concatenate | solution.py:376
  3.5 0.2 shard_map.68
  3.7 17.8 %all_to_all.40.gotm_ref = f32[8,32,128]{2,1,0:T(8,128)S(1)} all-to-all(f32[8,32,128]{2,1,0:T(8,128)S(1)} %get-tuple-element.18), channel_id=1, replica_groups=mesh['row'=32,'col'=8] {'col'}, dimensions={0} | all-to-all | bytes 262144 | tf_op jit(solution)/shard_map/all_to_all | solution.py:367
  21.5 16.7 %all_to_all.41.gotv_ref = f32[32,32,128]{2,1,0:T(8,128)S(1)} all-to-all(f32[32,32,128]{2,1,0:T(8,128)S(1)} %get-tuple-element.17), channel_id=1, replica_groups=mesh['row'=32,'col'=8] {'row'}, dimensions={0} | all-to-all | bytes 1048576 | tf_op jit(solution)/shard_map/all_to_all | solution.py:367
  38.2 15.6 %shard_map.69 = (bf16[12,448,1792]{2,1,0:T(8,128)(2,1)S(1)}, f32[448,1792]{1,0:T(8,128)S(1)}, f32[448,1792]{1,0:T(8,128)S(1)}, f32[4,448,128]{2,1,0:T(8,128)S(1)...) custom-call(f32[32,32,128]{2,1,0:T(8,128)S(1)} %all_to_all.41.gotv_ref, ...), custom_call_target="tpu_custom_call" | custom-call | flops 400000000 | bytes 1000000 | tf_op jit(solution)/shard_map/pallas_call | solution.py:333
  53.8 13.9 %all_to_all.42.got_ref = f32[8,32,128]{2,1,0:T(8,128)S(1)} all-to-all(f32[8,32,128]{2,1,0:T(8,128)S(1)} %get-tuple-element.20), channel_id=1, replica_groups=mesh['row'=32,'col'=8] {'col'}, dimensions={0} | all-to-all | bytes 262144 | tf_op jit(solution)/shard_map/all_to_all | solution.py:367
  67.7 0.1 shard_map.70
  67.8 11.5 %all_to_all.43.got_ref = f32[8,32,128]{2,1,0:T(8,128)S(1)} all-to-all(f32[8,32,128]{2,1,0:T(8,128)S(1)} %shard_map.70), channel_id=1, replica_groups=mesh['row'=32,'col'=8] {'col'}, dimensions={0} | all-to-all | bytes 262144 | tf_op jit(solution)/shard_map/all_to_all | solution.py:367
  79.4 0.0 copy-start
  79.4 0.0 copy-start.1
  79.4 3.1 %shard_map.71 = f32[32,24,128]{2,1,0:T(8,128)S(1)} custom-call(f32[8,32,128]{2,1,0:T(8,128)S(1)} %all_to_all.43.got_ref, bf16[12,448,1792]{2,1,0:T(8,128)(2,1)S(1)} %get-tuple-element.22.t_ref), custom_call_target="tpu_custom_call" | custom-call | flops 200000000 | bytes 1000000 | tf_op jit(solution)/shard_map/pallas_call | solution.py:342
  82.5 12.7 %all_to_all.44.got_ref = f32[32,24,128]{2,1,0:T(8,128)S(1)} all-to-all(f32[32,24,128]{2,1,0:T(8,128)S(1)} %shard_map.71), channel_id=1, replica_groups=mesh['row'=32,'col'=8] {'row'}, dimensions={0} | all-to-all | bytes 786432 | tf_op jit(solution)/shard_map/all_to_all | solution.py:367
  95.2 0.0 copy-done
  95.2 0.0 copy-done.1
  95.2 0.7 shard_map.72
  95.9 13.0 %all_to_all.45.got_ref = f32[32,32,128]{2,1,0:T(8,128)S(1)} all-to-all(f32[32,32,128]{2,1,0:T(8,128)S(1)} %get-tuple-element.24), channel_id=1, replica_groups=mesh['row'=32,'col'=8] {'row'}, dimensions={0} | all-to-all | bytes 1048576 | tf_op jit(solution)/shard_map/all_to_all | solution.py:367
  108.9 10.7 %shard_map.73 = (f32[8,8,128]{2,1,0:T(8,128)S(1)}, f32[32,8,128]{2,1,0:T(8,128)S(1)}) custom-call(f32[32,32,128]{2,1,0:T(8,128)S(1)} %all_to_all.45.got_ref, bf16[6,448,256]{2,1,0:T(8,128)(2,1)S(1)} %get-tuple-element.25.l_ref, f32[4,448,128]{2,1,0:T(8,128)S(1)} %get-tuple-element.26.xb_ref, f32[448,1792]{1,0:T(8,128)S(1)} %get-tuple-element.27.f5_ref, ...), custom_call_target="tpu_custom_call" | custom-call | flops 300000000 | bytes 1000000 | tf_op jit(solution)/shard_map/pallas_call | solution.py:359
  119.6 13.2 %all_to_all.46.rgot_ref = f32[8,8,128]{2,1,0:T(8,128)S(1)} all-to-all(f32[8,8,128]{2,1,0:T(8,128)S(1)} %get-tuple-element.30), channel_id=1, replica_groups=mesh['row'=32,'col'=8] {'col'}, dimensions={0} | all-to-all | bytes 65536 | tf_op jit(solution)/shard_map/all_to_all | solution.py:367
  132.8 10.9 %all_to_all.47.cgot_ref = f32[32,8,128]{2,1,0:T(8,128)S(1)} all-to-all(f32[32,8,128]{2,1,0:T(8,128)S(1)} %get-tuple-element.31), channel_id=1, replica_groups=mesh['row'=32,'col'=8] {'row'}, dimensions={0} | all-to-all | bytes 262144 | tf_op jit(solution)/shard_map/all_to_all | solution.py:367
  143.7 0.6 shard_map.74
  (2 shorter events, 0.0 us)
Async XLA Ops:
  79.4 15.8 %copy-start = (f32[3,16,56]{2,1,0:T(8,128)S(1)}, f32[3,16,56]{2,1,0:T(8,128)}, u32[]{:S(2)}) copy-start(f32[3,16,56]{2,1,0:T(8,128)} %param.7) | copy-start | bytes 32260
  79.4 15.8 %copy-start.1 = (f32[56]{0:T(128)S(1)}, f32[56]{0:T(128)}, u32[]{:S(2)}) copy-start(f32[56]{0:T(128)} %param.6) | copy-start | bytes 676

commit v4 on v3

--- a/solution.py
+++ b/solution.py
@@ -3,6 +3,7 @@
 from jax import lax
 from jax.experimental import pallas as pl
 from jax.experimental.pallas import tpu as pltpu
+from jax.sharding import Mesh
 from jax.sharding import PartitionSpec as P
 
 THOLE_DAMPING = 0.39
@@ -17,6 +18,11 @@
 CB = NROW * BEAD
 LANE = 128
 GEO = 48
+AXES = ("zl", "y", "x", "zh", "c")
+SIZES = (2, 4, 4, 4, 2)
+ROWS_OVER = ("zl", "zh")
+COLS_OVER = ("c", "y", "x")
+FREE = (53, 117)
 PAIRS = ((0, 0), (1, 1), (2, 2), (0, 1), (0, 2), (1, 2))
 VMEM_SPEC = pl.BlockSpec(memory_space=pltpu.VMEM)
 
@@ -55,7 +61,31 @@
         out_ref[j * BEAD + 32 : (j + 1) * BEAD, :] = pltpu.roll(piece[0:24], 64, 1)
 
 
-def prep_kernel(x_ref, own_ref, v_ref, mu_ref, mask_ref):
+def place():
+    return lax.axis_index("zh"), lax.axis_index("y") * 4 + lax.axis_index("x")
+
+
+def free_slot(lane):
+    left = (lane >= FREE[0]) & (lane < FREE[0] + 8)
+    right = (lane >= FREE[1]) & (lane < FREE[1] + 8)
+    return jnp.where(left, lane - FREE[0], jnp.where(right, lane - FREE[1] + 8, -1))
+
+
+def unpack_dense(got_ref, out_ref, blocks):
+    lanes = lane_ids((8, LANE))
+    for j in range(blocks):
+        piece = got_ref[j]
+        at = j * BEAD
+        out_ref[at : at + 24, :] = piece
+        out_ref[at + 24 : at + 48, :] = pltpu.roll(piece, 64, 1)
+        first, second, third = (
+            pltpu.roll(piece[8 * i : 8 * i + 8], 80 + 16 * i, 1) for i in range(3)
+        )
+        last = jnp.where(lanes < 16, first, jnp.where(lanes < 32, second, third))
+        out_ref[at + 48 : at + 56, :] = last
+
+
+def prep_kernel(x_ref, own_ref, mu_ref):
     pol = x_ref[99:100, :]
     row = lax.broadcasted_iota(jnp.int32, (16, BEAD), 0)
     geo = jnp.where(row == 3, lax.rsqrt(pol), jnp.where(row == 4, pol, 0.0))
@@ -68,15 +98,36 @@
     left = lane_ids((32, LANE)) < 64
     own = jnp.where(left, turned[0:32], swapped[32:64])
     own_ref[...] = own
-    for k in range(NROW):
-        v_ref[k] = own
     own = jnp.where(left, swapped[0:32], turned[32:64])
-    for k in range(NCOL):
-        mu_ref[k] = own
-    mask_ref[...] = x_ref[104:112, 0:NROW]
-
-
-def prepare_columns(got_ref, mask_ref, w_ref, xc_ref, m_ref, g_ref):
+    mask = x_ref[104:112, :].astype(BF16)
+    column = lax.broadcasted_iota(jnp.int32, (BEAD, LANE), 0)
+    slot = free_slot(lane_ids((BEAD, LANE)))
+    for zl in range(2):
+        chosen = ((slot >= 0) & (column == slot + 16 * zl)).astype(BF16)
+        part = own[0:8] + dot_f32(mask, chosen, ((1,), (0,)))
+        for zh in range(4):
+            mu_ref[zl * 4 + zh, 0:8, :] = part
+            mu_ref[zl * 4 + zh, 8:32, :] = own[8:32]
+
+
+def relay_kernel(got_ref, own_ref, v_ref):
+    zh = place()[0]
+    slot = free_slot(lane_ids((8, LANE)))
+    row = lax.broadcasted_iota(jnp.int32, (8, 8), 0)
+    source = lax.broadcasted_iota(jnp.int32, (8, 8), 1)
+    held = [jnp.where(slot >= 0, got_ref[zl * 4 + zh, 0:8, :], 0.0).astype(BF16) for zl in range(2)]
+    own = own_ref[...]
+    for core in range(2):
+        part = own[0:8]
+        for zl in range(2):
+            chosen = ((row // 4 == zl) & (source == (row % 4) * 2 + core)).astype(BF16)
+            part = part + dot_f32(chosen, held[zl], ((1,), (0,)))
+        for yx in range(16):
+            v_ref[core * 16 + yx, 0:8, :] = part
+            v_ref[core * 16 + yx, 8:32, :] = own[8:32]
+
+
+def prepare_columns(got_ref, w_ref, xc_ref, m_ref, g_ref):
     unpack(got_ref, g_ref, NROW)
     for k in range(CB // 256):
         rows = pl.ds(k * 256, 256)
@@ -86,10 +137,15 @@
         u = hi + pltpu.roll(lo, 64, 1)
         for n, (a, b) in enumerate(PAIRS):
             w_ref[n, rows, :] = arranged(u, a, b).astype(BF16)
-    block = lax.broadcasted_iota(jnp.int32, (NROW, CB), 1) // BEAD
-    owner = lax.broadcasted_iota(jnp.int32, (NROW, CB), 0)
-    chosen = (block == owner).astype(BF16)
-    keep_all = dot_f32(mask_ref[...].astype(BF16), chosen, ((1,), (0,)))
+    block = lax.broadcasted_iota(jnp.int32, (LANE, CB), 1) // BEAD
+    slot = free_slot(lax.broadcasted_iota(jnp.int32, (LANE, CB), 0))
+    here = place()[1]
+    keep_all = jnp.zeros((NCOL, CB), F32)
+    for core in range(2):
+        held = got_ref[core * 16 + here, 0:8, :]
+        held = jnp.where(free_slot(lane_ids((8, LANE))) >= 0, held, 0.0).astype(BF16)
+        chosen = (block == core * 16 + slot).astype(BF16)
+        keep_all = keep_all + dot_f32(held, chosen, ((1,), (0,)))
     for k in range(NCOL):
         m_ref[k] = jnp.broadcast_to(keep_all[k : k + 1], (8, CB))
 
@@ -107,7 +163,6 @@
 def build_kernel(
     gotv_ref,
     gotm_ref,
-    mask_ref,
     t_ref,
     f5_ref,
     g7_ref,
@@ -121,7 +176,7 @@
     w_ref,
     m_ref,
 ):
-    prepare_columns(gotv_ref, mask_ref, w_ref, xc_ref, m_ref, gc_ref)
+    prepare_columns(gotv_ref, w_ref, xc_ref, m_ref, gc_ref)
     unpack(gotm_ref, g_ref, NCOL)
     prepare_moments(l_ref, g_ref)
     for i in range(4):
@@ -225,8 +280,11 @@
     vec = pol_ref[...] * field
     vec = jnp.concatenate([vec, jnp.zeros((48, LANE - BEAD), F32)], axis=1)
     turned = jnp.concatenate([vec, jnp.zeros((LANE - 48, LANE), F32)], axis=0).T
-    left = lane_ids((32, LANE)) < 64
-    own = jnp.where(left, turned[0:32], pltpu.roll(turned[32:64], 64, 1))
+    lanes = lane_ids((24, LANE))
+    last = turned[48:56]
+    last = jnp.concatenate([pltpu.roll(last, shift, 1) for shift in (48, 32, 16)], axis=0)
+    own = jnp.where(lanes >= 64, pltpu.roll(turned[24:48], 64, 1), last)
+    own = jnp.where(lanes < 48, turned[0:24], own)
     for k in range(NROW):
         next_ref[k] = own
 
@@ -234,7 +292,7 @@
 def gradient_kernel(
     got_ref, l_ref, xb_ref, f5_ref, g7_ref, xc_ref, or_ref, oc_ref, g_ref, m_ref, h_ref, racc_ref, cacc_ref
 ):
-    unpack(got_ref, g_ref, NROW)
+    unpack_dense(got_ref, g_ref, NROW)
     for k in range(CB // 256):
         rows = pl.ds(k * 256, 256)
         hi, lo = hi_lo(vector_lanes(g_ref[rows, :]))
@@ -309,11 +367,14 @@
 
 
 def run_prep(x):
-    outs = [((32, LANE), F32), ((NROW, 32, LANE), F32), ((NCOL, 32, LANE), F32), ((NCOL, NROW), F32)]
-    return call(prep_kernel, outs, [], 100_000, 4)(x)
-
-
-def run_build(gotv, gotm, mask):
+    return call(prep_kernel, [((32, LANE), F32), ((NCOL, 32, LANE), F32)], [], 100_000, 4)(x)
+
+
+def run_relay(got, own):
+    return call(relay_kernel, [((NROW, 32, LANE), F32)], [], 100_000, 4)(got, own)[0]
+
+
+def run_build(gotv, gotm):
     outs = [
         ((12, RB, CB), BF16),
         ((RB, CB), F32),
@@ -330,7 +391,7 @@
         ((6, CB, LANE), BF16),
         ((NCOL, 8, CB), F32),
     ]
-    return call(build_kernel, outs, scratch, 400_000_000, 8)(gotv, gotm, mask)
+    return call(build_kernel, outs, scratch, 400_000_000, 8)(gotv, gotm)
 
 
 def run_first_own(got, v):
@@ -343,7 +404,7 @@
 
 
 def run_second_own(got, seeds, pol):
-    outs = [((48, BEAD), F32), ((NROW, 32, LANE), F32)]
+    outs = [((48, BEAD), F32), ((NROW, 24, LANE), F32)]
     return call(second_own_kernel, outs, [], 100_000, 4)(got, seeds, pol)
 
 
@@ -372,27 +433,22 @@
     pol = polarizability[None, :]
     mask = jnp.pad(tile_mask.astype(F32), ((0, 0), (0, BEAD - NROW)))
     blank = jnp.zeros((4, BEAD), F32)
-    own_v, all_v, all_mu, mask = run_prep(
+    own_v, all_mu = run_prep(
         jnp.concatenate([seeds, dipoles.reshape(48, BEAD), positions, pol, blank, mask], axis=0)
     )
-    got_v = exchange(all_v, "row")
-    got_mu = exchange(all_mu, "col")
-    t, f5, g7, xb, xc, moments, parts = run_build(got_v, got_mu, mask)
-    own_next = run_first_own(exchange(parts, "col"), own_v)
-    pieces = run_second(exchange(own_next, "col"), t)
-    field, own_adjoint = run_second_own(exchange(pieces, "row"), seeds, pol)
-    out_r, out_c = run_gradient(exchange(own_adjoint, "row"), moments, xb, f5, g7, xc)
-    gradient = run_final(exchange(out_r, "col"), exchange(out_c, "row"))
+    got_mu = exchange(all_mu, ROWS_OVER)
+    got_v = exchange(run_relay(got_mu, own_v), COLS_OVER)
+    t, f5, g7, xb, xc, moments, parts = run_build(got_v, got_mu)
+    own_next = run_first_own(exchange(parts, ROWS_OVER), own_v)
+    pieces = run_second(exchange(own_next, ROWS_OVER), t)
+    field, own_adjoint = run_second_own(exchange(pieces, COLS_OVER), seeds, pol)
+    out_r, out_c = run_gradient(exchange(own_adjoint, COLS_OVER), moments, xb, f5, g7, xc)
+    gradient = run_final(exchange(out_r, ROWS_OVER), exchange(out_c, COLS_OVER))
     return (field.reshape(3, 16, BEAD), gradient)
 
 
 def solution(mesh):
-    in_specs = (
-        P(None, ("row", "col")),
-        P(("row", "col")),
-        P(None, None, ("row", "col")),
-        P(None, None, ("row", "col")),
-        P("row", "col"),
-    )
-    out_specs = (P(None, None, ("row", "col")), P(None, ("row", "col")))
-    return jax.shard_map(local, mesh=mesh, in_specs=in_specs, out_specs=out_specs, check_vma=False)
+    named = Mesh(mesh.devices.reshape(SIZES), AXES)
+    in_specs = (P(None, AXES), P(AXES), P(None, None, AXES), P(None, None, AXES), P(AXES[:3], AXES[3:]))
+    out_specs = (P(None, None, AXES), P(None, AXES))
+    return jax.shard_map(local, mesh=named, in_specs=in_specs, out_specs=out_specs, check_vma=False)

time: 145 us -> 142 us (0.979)
  blocking collectives: 110 us -> 107 us
    all_to_all x8, blocking collectives: 110 us -> 107 us  [exchange(): return lax.all_to_all(x, axis, 0, 0, tiled=True)]
    pallas_call x2 -> x3, Pallas kernels: 15.8 us -> 16 us  [the longest x1 15.7 us: run_build(): return call(build_kernel, outs, scratch, 400000000, 8)(gotv, gotm)]
where the time goes in v4:
time: 142 us
  blocking collectives  107 us (75%)
  Pallas kernels  31.3 us (22%)
  local copies, waits for them, and re-layouts  2.19 us (2%)
    all_to_all x8, blocking collectives, exchange(): return lax.all_to_all(x, axis, 0, 0, tiled=True)  107 us
    pallas_call x1, Pallas kernels, run_build(): return call(build_kernel, outs, scratch, 400000000, 8)(gotv, gotm)  15.7 us
    pallas_call x1, Pallas kernels, run_gradient(): call(gradient_kernel, outs, scratch, 300000000, 12)(got, l, xb, f5, g7, xc)  10.8 us
    pallas_call x1, Pallas kernels, run_second(): call(second_kernel, [((NROW, 24, LANE), F32)], scratch, 200000000, 6)  3.1 us

profile of v4, /device:TPU:1, one launch (start us, length us, event | category | flops | bytes accessed | tf_op | source)
XLA Modules:
  0.0 141.8 jit_solution(17404945650460248358)
XLA Ops:
  0.6 0.7 convert_element_type.5
  1.3 2.2 %concatenate.3.x_ref = f32[112,56]{1,0:T(8,128)S(1)} concatenate(f32[48,56]{1,0:T(8,128)} %bitcast.4, f32[48,56]{1,0:T(8,128)} %bitcast.8, f32[3,56]{1,0:T(4,128)} %param.5, f32[1,56]{1,0:T(1,128)} %bitcast.6, f32[4,56]{1,0:T(4,128)S(1)} %broadcast_in_dim.7, f32[8,56]{1,0:T(8,128)S(1)} %pad.4), dimensions={0} | concatenate | bytes 50176 | tf_op jit(solution)/shard_map/concatenate | solution.py:437
  3.5 0.2 shard_map.68
  3.7 15.8 %all_to_all.40.got_ref.gotm_ref = f32[8,32,128]{2,1,0:T(8,128)S(1)} all-to-all(f32[8,32,128]{2,1,0:T(8,128)S(1)} %get-tuple-element.15), channel_id=1, replica_groups=mesh['zl'=2,'y'=4,'x'=4,'zh'=4,'c'=2] {'zl','zh'}, dimensions={0} | all-to-all | bytes 262144 | tf_op jit(solution)/shard_map/all_to_all | solution.py:428
  19.5 0.1 shard_map.69
  19.6 19.8 %all_to_all.41.gotv_ref = f32[32,32,128]{2,1,0:T(8,128)S(1)} all-to-all(f32[32,32,128]{2,1,0:T(8,128)S(1)} %shard_map.69), channel_id=1, replica_groups=mesh['zl'=2,'y'=4,'x'=4,'zh'=4,'c'=2] {'c','y','x'}, dimensions={0} | all-to-all | bytes 1048576 | tf_op jit(solution)/shard_map/all_to_all | solution.py:428
  39.5 15.7 %shard_map.70 = (bf16[12,448,1792]{2,1,0:T(8,128)(2,1)S(1)}, f32[448,1792]{1,0:T(8,128)S(1)}, f32[448,1792]{1,0:T(8,128)S(1)}, f32[4,448,128]{2,1,0:T(8,128)S(1)...) custom-call(f32[32,32,128]{2,1,0:T(8,128)S(1)} %all_to_all.41.gotv_ref, ...), custom_call_target="tpu_custom_call" | custom-call | flops 400000000 | bytes 1000000 | tf_op jit(solution)/shard_map/pallas_call | solution.py:394
  55.1 9.7 %all_to_all.42.got_ref = f32[8,32,128]{2,1,0:T(8,128)S(1)} all-to-all(f32[8,32,128]{2,1,0:T(8,128)S(1)} %get-tuple-element.17), channel_id=1, replica_groups=mesh['zl'=2,'y'=4,'x'=4,'zh'=4,'c'=2] {'zl','zh'}, dimensions={0} | all-to-all | bytes 262144 | tf_op jit(solution)/shard_map/all_to_all | solution.py:428
  64.9 0.1 shard_map.71
  65.0 9.7 %all_to_all.43.got_ref = f32[8,32,128]{2,1,0:T(8,128)S(1)} all-to-all(f32[8,32,128]{2,1,0:T(8,128)S(1)} %shard_map.71), channel_id=1, replica_groups=mesh['zl'=2,'y'=4,'x'=4,'zh'=4,'c'=2] {'zl','zh'}, dimensions={0} | all-to-all | bytes 262144 | tf_op jit(solution)/shard_map/all_to_all | solution.py:428
  74.6 0.0 copy-start
  74.6 0.0 copy-start.1
  74.6 3.1 %shard_map.72 = f32[32,24,128]{2,1,0:T(8,128)S(1)} custom-call(f32[8,32,128]{2,1,0:T(8,128)S(1)} %all_to_all.43.got_ref, bf16[12,448,1792]{2,1,0:T(8,128)(2,1)S(1)} %get-tuple-element.18.t_ref), custom_call_target="tpu_custom_call" | custom-call | flops 200000000 | bytes 1000000 | tf_op jit(solution)/shard_map/pallas_call | solution.py:403
  77.7 16.0 %all_to_all.44.got_ref = f32[32,24,128]{2,1,0:T(8,128)S(1)} all-to-all(f32[32,24,128]{2,1,0:T(8,128)S(1)} %shard_map.72), channel_id=1, replica_groups=mesh['zl'=2,'y'=4,'x'=4,'zh'=4,'c'=2] {'c','y','x'}, dimensions={0} | all-to-all | bytes 786432 | tf_op jit(solution)/shard_map/all_to_all | solution.py:428
  93.8 0.0 copy-done
  93.8 0.0 copy-done.1
  93.8 0.7 shard_map.73
  94.5 13.7 %all_to_all.45.got_ref = f32[32,24,128]{2,1,0:T(8,128)S(1)} all-to-all(f32[32,24,128]{2,1,0:T(8,128)S(1)} %get-tuple-element.20), channel_id=1, replica_groups=mesh['zl'=2,'y'=4,'x'=4,'zh'=4,'c'=2] {'c','y','x'}, dimensions={0} | all-to-all | bytes 786432 | tf_op jit(solution)/shard_map/all_to_all | solution.py:428
  108.2 10.8 %shard_map.74 = (f32[8,8,128]{2,1,0:T(8,128)S(1)}, f32[32,8,128]{2,1,0:T(8,128)S(1)}) custom-call(f32[32,24,128]{2,1,0:T(8,128)S(1)} %all_to_all.45.got_ref, bf16[6,448,256]{2,1,0:T(8,128)(2,1)S(1)} %get-tuple-element.21.l_ref, f32[4,448,128]{2,1,0:T(8,128)S(1)} %get-tuple-element.22.xb_ref, f32[448,1792]{1,0:T(8,128)S(1)} %get-tuple-element.23.f5_ref, ...), custom_call_target="tpu_custom_call" | custom-call | flops 300000000 | bytes 1000000 | tf_op jit(solution)/shard_map/pallas_call | solution.py:420
  119.0 9.1 %all_to_all.46.rgot_ref = f32[8,8,128]{2,1,0:T(8,128)S(1)} all-to-all(f32[8,8,128]{2,1,0:T(8,128)S(1)} %get-tuple-element.26), channel_id=1, replica_groups=mesh['zl'=2,'y'=4,'x'=4,'zh'=4,'c'=2] {'zl','zh'}, dimensions={0} | all-to-all | bytes 65536 | tf_op jit(solution)/shard_map/all_to_all | solution.py:428
  128.0 13.1 %all_to_all.47.cgot_ref = f32[32,8,128]{2,1,0:T(8,128)S(1)} all-to-all(f32[32,8,128]{2,1,0:T(8,128)S(1)} %get-tuple-element.27), channel_id=1, replica_groups=mesh['zl'=2,'y'=4,'x'=4,'zh'=4,'c'=2] {'c','y','x'}, dimensions={0} | all-to-all | bytes 262144 | tf_op jit(solution)/shard_map/all_to_all | solution.py:428
  141.2 0.6 shard_map.75
  (2 shorter events, 0.0 us)
Async XLA Ops:
  74.6 19.1 %copy-start = (f32[3,16,56]{2,1,0:T(8,128)S(1)}, f32[3,16,56]{2,1,0:T(8,128)}, u32[]{:S(2)}) copy-start(f32[3,16,56]{2,1,0:T(8,128)} %param.7) | copy-start | bytes 32260
  74.6 19.1 %copy-start.1 = (f32[56]{0:T(128)S(1)}, f32[56]{0:T(128)}, u32[]{:S(2)}) copy-start(f32[56]{0:T(128)} %param.6) | copy-start | bytes 676

commit v5 on v4

--- a/solution.py
+++ b/solution.py
@@ -52,6 +52,21 @@
     down = pltpu.roll(u, LANE - step, 1)
     up = pltpu.roll(u, step, 1)
     return jnp.where(group == a, down, jnp.where(group == b, up, 0.0))
+
+
+def arranged_rows(vec, w_ref, cols):
+    hi, lo = hi_lo(vec)
+    u = jnp.concatenate([hi, lo], axis=0)
+    group = (lax.broadcasted_iota(jnp.int32, u.shape, 0) % 48) // 16
+    for n, (a, b) in enumerate(PAIRS):
+        if a == b:
+            w = jnp.where(group == a, u, 0.0)
+        else:
+            step = 16 * (b - a)
+            down = jnp.concatenate([u[step:], u[:step]], axis=0)
+            up = jnp.concatenate([u[96 - step :], u[: 96 - step]], axis=0)
+            w = jnp.where(group == a, down, jnp.where(group == b, up, 0.0))
+        w_ref[n, :, cols] = w.astype(BF16)
 
 
 def unpack(got_ref, out_ref, blocks):
@@ -130,13 +145,10 @@
 def prepare_columns(got_ref, w_ref, xc_ref, m_ref, g_ref):
     unpack(got_ref, g_ref, NROW)
     for k in range(CB // 256):
-        rows = pl.ds(k * 256, 256)
-        g = g_ref[rows, :]
-        xc_ref[:, rows] = g.T[GEO : GEO + 8]
-        hi, lo = hi_lo(vector_lanes(g))
-        u = hi + pltpu.roll(lo, 64, 1)
-        for n, (a, b) in enumerate(PAIRS):
-            w_ref[n, rows, :] = arranged(u, a, b).astype(BF16)
+        cols = pl.ds(k * 256, 256)
+        turned = g_ref[cols, :].T
+        xc_ref[:, cols] = turned[GEO : GEO + 8]
+        arranged_rows(turned[0:48], w_ref, cols)
     block = lax.broadcasted_iota(jnp.int32, (LANE, CB), 1) // BEAD
     slot = free_slot(lax.broadcasted_iota(jnp.int32, (LANE, CB), 0))
     here = place()[1]
@@ -217,10 +229,11 @@
         return carry
 
     lax.fori_loop(0, RB // 16, row_chunk, 0)
-    total = dot_f32(t_ref[0], w_ref[0], ((1,), (0,)))
+    total = dot_f32(w_ref[0], t_ref[0], ((1,), (1,)))
     for n in range(1, 12):
-        total += dot_f32(t_ref[n], w_ref[n % 6], ((1,), (0,)))
-    y_ref[...] = total + pltpu.roll(total, 64, 1)
+        total += dot_f32(w_ref[n % 6], t_ref[n], ((1,), (1,)))
+    half = jnp.concatenate([total[0:48] + total[48:96], jnp.zeros((16, RB), F32)], axis=0)
+    y_ref[...] = jnp.concatenate([half, half], axis=0).T
     left = lane_ids((24, LANE)) < 64
     for k in range(NCOL):
         at = k * BEAD
@@ -246,19 +259,7 @@
 
 def second_kernel(got_ref, t_ref, out_ref, g_ref, w_ref, y_ref):
     unpack(got_ref, g_ref, NCOL)
-    hi, lo = hi_lo(vector_lanes(g_ref[...]))
-    ut = (hi + pltpu.roll(lo, 64, 1)).T
-    ut = jnp.concatenate([ut[0:48], ut[64:112]], axis=0)
-    group = (lax.broadcasted_iota(jnp.int32, (96, RB), 0) % 48) // 16
-    for n, (a, b) in enumerate(PAIRS):
-        if a == b:
-            w = jnp.where(group == a, ut, 0.0)
-        else:
-            step = 16 * (b - a)
-            down = jnp.concatenate([ut[step:], ut[:step]], axis=0)
-            up = jnp.concatenate([ut[96 - step :], ut[: 96 - step]], axis=0)
-            w = jnp.where(group == a, down, jnp.where(group == b, up, 0.0))
-        w_ref[n] = w.astype(BF16)
+    arranged_rows(g_ref[...].T[0:48], w_ref, slice(None))
     for k in range(7):
         cols = pl.ds(k * 256, 256)
         total = jnp.zeros((96, 256), F32)
@@ -388,7 +389,7 @@
         ((CB, LANE), F32),
         ((RB, LANE), F32),
         ((RB, LANE), F32),
-        ((6, CB, LANE), BF16),
+        ((6, 96, CB), BF16),
         ((NCOL, 8, CB), F32),
     ]
     return call(build_kernel, outs, scratch, 400_000_000, 8)(gotv, gotm)

time: 142 us -> 142 us (level)
  no operation moved by 1% of the time
where the time goes in v5:
time: 142 us
  blocking collectives  107 us (75%)
  Pallas kernels  31 us (22%)
  local copies, waits for them, and re-layouts  2.19 us (2%)
    all_to_all x8, blocking collectives, exchange(): return lax.all_to_all(x, axis, 0, 0, tiled=True)  107 us
    pallas_call x1, Pallas kernels, run_build(): return call(build_kernel, outs, scratch, 400000000, 8)(gotv, gotm)  15.5 us
    pallas_call x1, Pallas kernels, run_gradient(): call(gradient_kernel, outs, scratch, 300000000, 12)(got, l, xb, f5, g7, xc)  10.8 us
    pallas_call x1, Pallas kernels, run_second(): call(second_kernel, [((NROW, 24, LANE), F32)], scratch, 200000000, 6)  3.03 us

profile of v5, /device:TPU:1, one launch (start us, length us, event | category | flops | bytes accessed | tf_op | source)
XLA Modules:
  0.0 141.5 jit_solution(15525078863225830695)
XLA Ops:
  0.6 0.7 convert_element_type.5
  1.3 2.2 %concatenate.3.x_ref = f32[112,56]{1,0:T(8,128)S(1)} concatenate(f32[48,56]{1,0:T(8,128)} %bitcast.4, f32[48,56]{1,0:T(8,128)} %bitcast.8, f32[3,56]{1,0:T(4,128)} %param.5, f32[1,56]{1,0:T(1,128)} %bitcast.6, f32[4,56]{1,0:T(4,128)S(1)} %broadcast_in_dim.7, f32[8,56]{1,0:T(8,128)S(1)} %pad.4), dimensions={0} | concatenate | bytes 50176 | tf_op jit(solution)/shard_map/concatenate | solution.py:438
  3.5 0.2 shard_map.68
  3.7 15.8 %all_to_all.40.got_ref.gotm_ref = f32[8,32,128]{2,1,0:T(8,128)S(1)} all-to-all(f32[8,32,128]{2,1,0:T(8,128)S(1)} %get-tuple-element.15), channel_id=1, replica_groups=mesh['zl'=2,'y'=4,'x'=4,'zh'=4,'c'=2] {'zl','zh'}, dimensions={0} | all-to-all | bytes 262144 | tf_op jit(solution)/shard_map/all_to_all | solution.py:429
  19.5 0.1 shard_map.69
  19.6 19.8 %all_to_all.41.gotv_ref = f32[32,32,128]{2,1,0:T(8,128)S(1)} all-to-all(f32[32,32,128]{2,1,0:T(8,128)S(1)} %shard_map.69), channel_id=1, replica_groups=mesh['zl'=2,'y'=4,'x'=4,'zh'=4,'c'=2] {'c','y','x'}, dimensions={0} | all-to-all | bytes 1048576 | tf_op jit(solution)/shard_map/all_to_all | solution.py:429
  39.5 15.5 %shard_map.70 = (bf16[12,448,1792]{2,1,0:T(8,128)(2,1)S(1)}, f32[448,1792]{1,0:T(8,128)S(1)}, f32[448,1792]{1,0:T(8,128)S(1)}, f32[4,448,128]{2,1,0:T(8,128)S(1)...) custom-call(f32[32,32,128]{2,1,0:T(8,128)S(1)} %all_to_all.41.gotv_ref, ...), custom_call_target="tpu_custom_call" | custom-call | flops 400000000 | bytes 1000000 | tf_op jit(solution)/shard_map/pallas_call | solution.py:395
  55.0 9.7 %all_to_all.42.got_ref = f32[8,32,128]{2,1,0:T(8,128)S(1)} all-to-all(f32[8,32,128]{2,1,0:T(8,128)S(1)} %get-tuple-element.17), channel_id=1, replica_groups=mesh['zl'=2,'y'=4,'x'=4,'zh'=4,'c'=2] {'zl','zh'}, dimensions={0} | all-to-all | bytes 262144 | tf_op jit(solution)/shard_map/all_to_all | solution.py:429
  64.7 0.1 shard_map.71
  64.8 9.7 %all_to_all.43.got_ref = f32[8,32,128]{2,1,0:T(8,128)S(1)} all-to-all(f32[8,32,128]{2,1,0:T(8,128)S(1)} %shard_map.71), channel_id=1, replica_groups=mesh['zl'=2,'y'=4,'x'=4,'zh'=4,'c'=2] {'zl','zh'}, dimensions={0} | all-to-all | bytes 262144 | tf_op jit(solution)/shard_map/all_to_all | solution.py:429
  74.5 0.0 copy-start
  74.5 0.0 copy-start.1
  74.5 3.0 %shard_map.72 = f32[32,24,128]{2,1,0:T(8,128)S(1)} custom-call(f32[8,32,128]{2,1,0:T(8,128)S(1)} %all_to_all.43.got_ref, bf16[12,448,1792]{2,1,0:T(8,128)(2,1)S(1)} %get-tuple-element.18.t_ref), custom_call_target="tpu_custom_call" | custom-call | flops 200000000 | bytes 1000000 | tf_op jit(solution)/shard_map/pallas_call | solution.py:404
  77.5 16.0 %all_to_all.44.got_ref = f32[32,24,128]{2,1,0:T(8,128)S(1)} all-to-all(f32[32,24,128]{2,1,0:T(8,128)S(1)} %shard_map.72), channel_id=1, replica_groups=mesh['zl'=2,'y'=4,'x'=4,'zh'=4,'c'=2] {'c','y','x'}, dimensions={0} | all-to-all | bytes 786432 | tf_op jit(solution)/shard_map/all_to_all | solution.py:429
  93.5 0.0 copy-done
  93.5 0.0 copy-done.1
  93.5 0.7 shard_map.73
  94.3 13.7 %all_to_all.45.got_ref = f32[32,24,128]{2,1,0:T(8,128)S(1)} all-to-all(f32[32,24,128]{2,1,0:T(8,128)S(1)} %get-tuple-element.20), channel_id=1, replica_groups=mesh['zl'=2,'y'=4,'x'=4,'zh'=4,'c'=2] {'c','y','x'}, dimensions={0} | all-to-all | bytes 786432 | tf_op jit(solution)/shard_map/all_to_all | solution.py:429
  107.9 10.8 %shard_map.74 = (f32[8,8,128]{2,1,0:T(8,128)S(1)}, f32[32,8,128]{2,1,0:T(8,128)S(1)}) custom-call(f32[32,24,128]{2,1,0:T(8,128)S(1)} %all_to_all.45.got_ref, bf16[6,448,256]{2,1,0:T(8,128)(2,1)S(1)} %get-tuple-element.21.l_ref, f32[4,448,128]{2,1,0:T(8,128)S(1)} %get-tuple-element.22.xb_ref, f32[448,1792]{1,0:T(8,128)S(1)} %get-tuple-element.23.f5_ref, ...), custom_call_target="tpu_custom_call" | custom-call | flops 300000000 | bytes 1000000 | tf_op jit(solution)/shard_map/pallas_call | solution.py:421
  118.7 9.1 %all_to_all.46.rgot_ref = f32[8,8,128]{2,1,0:T(8,128)S(1)} all-to-all(f32[8,8,128]{2,1,0:T(8,128)S(1)} %get-tuple-element.26), channel_id=1, replica_groups=mesh['zl'=2,'y'=4,'x'=4,'zh'=4,'c'=2] {'zl','zh'}, dimensions={0} | all-to-all | bytes 65536 | tf_op jit(solution)/shard_map/all_to_all | solution.py:429
  127.8 13.1 %all_to_all.47.cgot_ref = f32[32,8,128]{2,1,0:T(8,128)S(1)} all-to-all(f32[32,8,128]{2,1,0:T(8,128)S(1)} %get-tuple-element.27), channel_id=1, replica_groups=mesh['zl'=2,'y'=4,'x'=4,'zh'=4,'c'=2] {'c','y','x'}, dimensions={0} | all-to-all | bytes 262144 | tf_op jit(solution)/shard_map/all_to_all | solution.py:429
  140.9 0.6 shard_map.75
  (2 shorter events, 0.0 us)
Async XLA Ops:
  74.5 19.1 %copy-start = (f32[3,16,56]{2,1,0:T(8,128)S(1)}, f32[3,16,56]{2,1,0:T(8,128)}, u32[]{:S(2)}) copy-start(f32[3,16,56]{2,1,0:T(8,128)} %param.7) | copy-start | bytes 32260
  74.5 19.1 %copy-start.1 = (f32[56]{0:T(128)S(1)}, f32[56]{0:T(128)}, u32[]{:S(2)}) copy-start(f32[56]{0:T(128)} %param.6) | copy-start | bytes 676

commit v6 on v5

--- a/solution.py
+++ b/solution.py
@@ -432,10 +432,10 @@
 def local(positions, polarizability, seeds, dipoles, tile_mask):
     seeds = seeds.reshape(48, BEAD)
     pol = polarizability[None, :]
-    mask = jnp.pad(tile_mask.astype(F32), ((0, 0), (0, BEAD - NROW)))
-    blank = jnp.zeros((4, BEAD), F32)
+    placed = ((seeds, 0), (dipoles.reshape(48, BEAD), 48), (positions, 96), (pol, 99))
+    placed += ((tile_mask.astype(F32), 104),)
     own_v, all_mu = run_prep(
-        jnp.concatenate([seeds, dipoles.reshape(48, BEAD), positions, pol, blank, mask], axis=0)
+        sum(jnp.pad(x, ((at, 112 - at - x.shape[0]), (0, BEAD - x.shape[1]))) for x, at in placed)
     )
     got_mu = exchange(all_mu, ROWS_OVER)
     got_v = exchange(run_relay(got_mu, own_v), COLS_OVER)

time: 142 us -> 141 us (level)
  local copies, waits for them, and re-layouts: 2.19 us -> 0.01 us
    concatenate x1 -> x0, local copies, waits for them, and re-layouts: 2.18 us -> none  [local(): jnp.concatenate([seeds, dipoles.reshape(48, BEAD), positions, pol, blank,...]
where the time goes in v6:
time: 141 us; the launch traced here: 140 us
  blocking collectives  107 us (76%)
  Pallas kernels  31 us (22%)
  other arithmetic  1.49 us (1%)
    all_to_all x8, blocking collectives, exchange(): return lax.all_to_all(x, axis, 0, 0, tiled=True)  107 us
    pallas_call x1, Pallas kernels, run_build(): return call(build_kernel, outs, scratch, 400000000, 8)(gotv, gotm)  15.5 us
    pallas_call x1, Pallas kernels, run_gradient(): call(gradient_kernel, outs, scratch, 300000000, 12)(got, l, xb, f5, g7, xc)  10.8 us
    pallas_call x1, Pallas kernels, run_second(): call(second_kernel, [((NROW, 24, LANE), F32)], scratch, 200000000, 6)  3.03 us

profile of v6, /device:TPU:1, one launch (start us, length us, event | category | flops | bytes accessed | tf_op | source)
XLA Modules:
  0.0 140.2 jit_solution(1264403903313670641)
XLA Ops:
  0.6 0.7 convert_element_type.13
  1.3 0.8 pad_add_fusion.x_ref
  2.1 0.2 shard_map.68
  2.3 15.8 %all_to_all.40.got_ref.gotm_ref = f32[8,32,128]{2,1,0:T(8,128)S(1)} all-to-all(f32[8,32,128]{2,1,0:T(8,128)S(1)} %get-tuple-element.15), channel_id=1, replica_groups=mesh['zl'=2,'y'=4,'x'=4,'zh'=4,'c'=2] {'zl','zh'}, dimensions={0} | all-to-all | bytes 262144 | tf_op jit(solution)/shard_map/all_to_all | solution.py:429
  18.1 0.1 shard_map.69
  18.3 19.8 %all_to_all.41.gotv_ref = f32[32,32,128]{2,1,0:T(8,128)S(1)} all-to-all(f32[32,32,128]{2,1,0:T(8,128)S(1)} %shard_map.69), channel_id=1, replica_groups=mesh['zl'=2,'y'=4,'x'=4,'zh'=4,'c'=2] {'c','y','x'}, dimensions={0} | all-to-all | bytes 1048576 | tf_op jit(solution)/shard_map/all_to_all | solution.py:429
  38.1 15.5 %shard_map.70 = (bf16[12,448,1792]{2,1,0:T(8,128)(2,1)S(1)}, f32[448,1792]{1,0:T(8,128)S(1)}, f32[448,1792]{1,0:T(8,128)S(1)}, f32[4,448,128]{2,1,0:T(8,128)S(1)...) custom-call(f32[32,32,128]{2,1,0:T(8,128)S(1)} %all_to_all.41.gotv_ref, ...), custom_call_target="tpu_custom_call" | custom-call | flops 400000000 | bytes 1000000 | tf_op jit(solution)/shard_map/pallas_call | solution.py:395
  53.6 9.7 %all_to_all.42.got_ref = f32[8,32,128]{2,1,0:T(8,128)S(1)} all-to-all(f32[8,32,128]{2,1,0:T(8,128)S(1)} %get-tuple-element.17), channel_id=1, replica_groups=mesh['zl'=2,'y'=4,'x'=4,'zh'=4,'c'=2] {'zl','zh'}, dimensions={0} | all-to-all | bytes 262144 | tf_op jit(solution)/shard_map/all_to_all | solution.py:429
  63.3 0.1 shard_map.71
  63.4 9.7 %all_to_all.43.got_ref = f32[8,32,128]{2,1,0:T(8,128)S(1)} all-to-all(f32[8,32,128]{2,1,0:T(8,128)S(1)} %shard_map.71), channel_id=1, replica_groups=mesh['zl'=2,'y'=4,'x'=4,'zh'=4,'c'=2] {'zl','zh'}, dimensions={0} | all-to-all | bytes 262144 | tf_op jit(solution)/shard_map/all_to_all | solution.py:429
  73.1 0.0 copy-start
  73.1 0.0 copy-start.1
  73.1 3.0 %shard_map.72 = f32[32,24,128]{2,1,0:T(8,128)S(1)} custom-call(f32[8,32,128]{2,1,0:T(8,128)S(1)} %all_to_all.43.got_ref, bf16[12,448,1792]{2,1,0:T(8,128)(2,1)S(1)} %get-tuple-element.18.t_ref), custom_call_target="tpu_custom_call" | custom-call | flops 200000000 | bytes 1000000 | tf_op jit(solution)/shard_map/pallas_call | solution.py:404
  76.1 16.0 %all_to_all.44.got_ref = f32[32,24,128]{2,1,0:T(8,128)S(1)} all-to-all(f32[32,24,128]{2,1,0:T(8,128)S(1)} %shard_map.72), channel_id=1, replica_groups=mesh['zl'=2,'y'=4,'x'=4,'zh'=4,'c'=2] {'c','y','x'}, dimensions={0} | all-to-all | bytes 786432 | tf_op jit(solution)/shard_map/all_to_all | solution.py:429
  92.1 0.0 copy-done
  92.1 0.0 copy-done.1
  92.1 0.7 shard_map.73
  92.9 13.7 %all_to_all.45.got_ref = f32[32,24,128]{2,1,0:T(8,128)S(1)} all-to-all(f32[32,24,128]{2,1,0:T(8,128)S(1)} %get-tuple-element.20), channel_id=1, replica_groups=mesh['zl'=2,'y'=4,'x'=4,'zh'=4,'c'=2] {'c','y','x'}, dimensions={0} | all-to-all | bytes 786432 | tf_op jit(solution)/shard_map/all_to_all | solution.py:429
  106.5 10.8 %shard_map.74 = (f32[8,8,128]{2,1,0:T(8,128)S(1)}, f32[32,8,128]{2,1,0:T(8,128)S(1)}) custom-call(f32[32,24,128]{2,1,0:T(8,128)S(1)} %all_to_all.45.got_ref, bf16[6,448,256]{2,1,0:T(8,128)(2,1)S(1)} %get-tuple-element.21.l_ref, f32[4,448,128]{2,1,0:T(8,128)S(1)} %get-tuple-element.22.xb_ref, f32[448,1792]{1,0:T(8,128)S(1)} %get-tuple-element.23.f5_ref, ...), custom_call_target="tpu_custom_call" | custom-call | flops 300000000 | bytes 1000000 | tf_op jit(solution)/shard_map/pallas_call | solution.py:421
  117.3 9.1 %all_to_all.46.rgot_ref = f32[8,8,128]{2,1,0:T(8,128)S(1)} all-to-all(f32[8,8,128]{2,1,0:T(8,128)S(1)} %get-tuple-element.26), channel_id=1, replica_groups=mesh['zl'=2,'y'=4,'x'=4,'zh'=4,'c'=2] {'zl','zh'}, dimensions={0} | all-to-all | bytes 65536 | tf_op jit(solution)/shard_map/all_to_all | solution.py:429
  126.4 13.1 %all_to_all.47.cgot_ref = f32[32,8,128]{2,1,0:T(8,128)S(1)} all-to-all(f32[32,8,128]{2,1,0:T(8,128)S(1)} %get-tuple-element.27), channel_id=1, replica_groups=mesh['zl'=2,'y'=4,'x'=4,'zh'=4,'c'=2] {'c','y','x'}, dimensions={0} | all-to-all | bytes 262144 | tf_op jit(solution)/shard_map/all_to_all | solution.py:429
  139.5 0.6 shard_map.75
Async XLA Ops:
  73.1 19.1 %copy-start = (f32[3,16,56]{2,1,0:T(8,128)S(1)}, f32[3,16,56]{2,1,0:T(8,128)}, u32[]{:S(2)}) copy-start(f32[3,16,56]{2,1,0:T(8,128)} %param.7) | copy-start | bytes 32260
  73.1 19.1 %copy-start.1 = (f32[56]{0:T(128)S(1)}, f32[56]{0:T(128)}, u32[]{:S(2)}) copy-start(f32[56]{0:T(128)} %param.6) | copy-start | bytes 676
